TPU v7x, 256 devices: a whole 4x4x8 slice. The times are simulated.
256 devices in a mesh: grow: 16 (over z_lo, x), wide: 16 (over z_hi, y, core).
Axes of the slice: x: 4, y: 4, z: 8 (z_hi: 2, z_lo: 4; z = z_hi * 4 + z_lo), core: 2. Of those that a mesh axis runs over, the one named last changes fastest.
Arguments:
- fields: float32 [3, 256, 512, 128], P(None, 'grow', 'wide'), may hold values from -1 to 1
- melt_planes: float32 [3, 16, 512, 128], P(None, None, 'wide'), may hold values from -1 to 1
- slide_planes: int32 [8], replicated, may hold values from 0 to 8, as said below
Outputs:
- evolved: float32 [3, 256, 512, 128], P(None, 'grow', 'wide')
Inputs may be any that keep to these rules, and one draw needn't show every extreme that they name: `slide_planes`: entries at even positions k are 0; at least one entry equals 8, and at most one other entry is nonzero.
All inputs are finite; a program needn't handle non-finite values.
Results may differ from a plain program's by a relative error of at most 0.0001.
Values sent between devices are 32-bit elements; how exact they have to be, the bound alone decides.
A program may use at most 64 MiB of HBM per device.

v0:
```python
import jax
import jax.numpy as jnp
from jax import lax
from jax.sharding import PartitionSpec as P

SUBSTEPS = 8


coef_phase = 0.15
coef_react = 0.3
coef_couple = 0.4
coef_solute = 1.5
coef_diff = 0.1
coef_heat = 0.16


def passed_along(value, axis, steps):
    count = lax.axis_size(axis)
    leading, last = (max(0, -steps), min(count, count - steps))
    return lax.ppermute(value, axis, [(source, source + steps) for source in range(leading, last)])


def with_halo(block, sides, width):
    for axis, dim in sides:
        count = lax.axis_size(axis)
        forward = [(i, i + 1) for i in range(count - 1)]
        backward = [(target, source) for source, target in forward]
        low = lax.ppermute(
            lax.slice_in_dim(block, block.shape[dim] - width, None, axis=dim), axis, forward
        )
        high = lax.ppermute(lax.slice_in_dim(block, 0, width, axis=dim), axis, backward)
        block = jnp.concatenate([low, block, high], axis=dim)
    return block


def advance(padded):
    centre = padded[:, 1:-1, 1:-1]
    laplace = (
        padded[:, 2:, 1:-1]
        + padded[:, :-2, 1:-1]
        + padded[:, 1:-1, 2:]
        + padded[:, 1:-1, :-2]
        + jnp.roll(centre, 1, 3)
        + jnp.roll(centre, -1, 3)
        - 6.0 * centre
    )
    phase_now, solute, thermal = (centre[0], centre[1], centre[2])
    squared = 1.0 - phase_now * phase_now
    driving = (
        phase_now
        + coef_phase * laplace[0]
        + coef_react * (phase_now - phase_now * phase_now * phase_now)
        - coef_couple * squared * squared * (thermal + coef_solute * solute)
    )
    grown = jnp.tanh(driving)
    change = 0.5 * (grown - phase_now)
    solute_next = solute + coef_diff * laplace[1] + change
    thermal_next = thermal + coef_heat * laplace[2] + change
    return jnp.stack([grown, solute_next, thermal_next])


def inside_mask(rows, cols):
    grow_total = rows * lax.axis_size("grow")
    wide_total = cols * lax.axis_size("wide")
    grow_index = lax.axis_index("grow") * rows - 1 + jnp.arange(rows + 2, dtype=jnp.int32)
    wide_index = lax.axis_index("wide") * cols - 1 + jnp.arange(cols + 2, dtype=jnp.int32)
    grow_inside = (grow_index >= 0) & (grow_index < grow_total)
    wide_inside = (wide_index >= 0) & (wide_index < wide_total)
    inside = (grow_inside[:, None] & wide_inside[None, :]).astype(jnp.float32)
    return inside[None, :, :, None]


def slide_block(state, melt_planes, shift, cursor):
    rows = state.shape[1]
    at_end = lax.axis_index("grow") == lax.axis_size("grow") - 1
    doubled = jnp.concatenate([melt_planes, melt_planes], 1)
    melt_piece = lax.dynamic_slice_in_dim(doubled, cursor, rows, 1)
    received = passed_along(state, "grow", -1)
    incoming = jnp.where(at_end, melt_piece, received)
    combined = jnp.concatenate([state, incoming], 1)
    return lax.dynamic_slice_in_dim(combined, shift, rows, 1)


def body(fields, melt_planes, slide_planes):
    rows = fields.shape[1]
    cols = fields.shape[2]
    state = fields
    inside = inside_mask(rows, cols)
    for pair_index in range(SUBSTEPS // 2):
        padded = with_halo(state, (("grow", 1), ("wide", 2)), 2)
        middle = advance(padded) * inside
        state = advance(middle)
        substep = 2 * pair_index + 1
        shift = slide_planes[substep]
        cursor = jnp.sum(slide_planes[:substep])
        state = slide_block(state, melt_planes, shift, cursor)
    return state


def solution(mesh):
    return jax.shard_map(
        body,
        mesh=mesh,
        in_specs=(P(None, "grow", "wide", None), P(None, None, "wide", None), P()),
        out_specs=P(None, "grow", "wide", None),
        check_vma=False,
    )
```

profile of v0, /device:TPU:224, one launch (start us, length us, event | category | flops | bytes accessed | tf_op | source)
XLA Modules:
  0.0 196.0 jit_solution(3952511474066303948)
XLA Ops:
  0.0 1.0 fusion.152
  1.0 3.4 %collective-permute-start = (f32[3,2,32,128]{3,2,1,0:T(8,128)S(1)}, f32[3,2,32,128]{3,2,1,0:T(8,128)S(1)}, u32[]{:S(2)}, u32[]{:S(2)}) collective-permute-start(f32[3,2,32,128]{3,2,1,0:T(8,128)S(1)} %get-tuple-element.68), channel_id=1, source_target_pairs={{0,16},{16,32},{32,48},{48,64},{64,80},{80,96},{96,112},{112,128},... | collective-permute-start | bytes 294920 | tf_op jit(solution)/shard_map/ppermute | solution.py:28
  4.4 4.6 %collective-permute-start.1 = (f32[3,2,32,128]{3,2,1,0:T(8,128)S(1)}, f32[3,2,32,128]{3,2,1,0:T(8,128)S(1)}, u32[]{:S(2)}, u32[]{:S(2)}) collective-permute-start(f32[3,2,32,128]{3,2,1,0:T(8,128)S(1)} %get-tuple-element.67), channel_id=1, source_target_pairs={{16,0},{32,16},{48,32},{64,48},{80,64},{96,80},{112,96},{128,112},... | collective-permute-start | bytes 294920 | tf_op jit(solution)/shard_map/ppermute | solution.py:31
  9.0 0.6 collective-permute-done
  9.6 1.2 constant_dynamic-update-slice_fusion.1
  10.8 0.3 collective-permute-done.1
  11.2 4.1 %collective-permute-start.3 = (f32[3,20,2,128]{3,2,1,0:T(2,128)S(1)}, f32[3,20,2,128]{3,2,1,0:T(2,128)S(1)}, u32[]{:S(2)}, u32[]{:S(2)}) collective-permute-start(f32[3,20,2,128]{3,2,1,0:T(2,128)S(1)} %get-tuple-element.60), channel_id=1, source_target_pairs={{1,0},{2,1},{3,2},{4,3},{5,4},{6,5},{7,6},{8,7},{9,8},{10,9},{11,1... | collective-permute-start | bytes 184328 | tf_op jit(solution)/shard_map/ppermute | solution.py:31
  15.3 1.9 collective-permute-start.2
  17.3 9.6 %collective-permute-done.2 = f32[3,20,2,128]{3,2,1,0:T(2,128)S(1)} collective-permute-done((f32[3,20,2,128]{3,2,1,0:T(2,128)S(1)}, f32[3,20,2,128]{3,2,1,0:T(2,128)S(1)}, u32[]{:S(2)}, u32[]{:S(2)}) %collective-permute-start.2) | collective-permute-done | bytes 61472 | tf_op jit(solution)/shard_map/ppermute | solution.py:28
  27.0 0.4 fusion.138
  27.4 0.4 fusion.139
  27.8 0.9 fusion.15
  28.7 0.3 fusion.82
  29.9 0.6 fusion.41
  31.0 0.9 pad_maximum_fusion.24
  31.9 6.1 %collective-permute-start.4 = (f32[3,16,32,128]{3,2,1,0:T(8,128)}, f32[3,16,32,128]{3,2,1,0:T(8,128)}, u32[]{:S(2)}, u32[]{:S(2)}) collective-permute-start(f32[3,16,32,128]{3,2,1,0:T(8,128)} %pad_maximum_fusion.24), channel_id=1, source_target_pairs={{16,0},{32,16},{48,32},{64,48},{80,64},{96,80},{112,96},{128,112},... | collective-permute-start | bytes 2359304 | tf_op jit(solution)/shard_map/ppermute | solution.py:20
  38.0 0.7 fusion.153
  42.6 6.2 %collective-permute-done.4 = f32[3,16,32,128]{3,2,1,0:T(8,128)} collective-permute-done((f32[3,16,32,128]{3,2,1,0:T(8,128)}, f32[3,16,32,128]{3,2,1,0:T(8,128)}, u32[]{:S(2)}, u32[]{:S(2)}) %collective-permute-start.4) | collective-permute-done | bytes 786464 | tf_op jit(solution)/shard_map/ppermute | solution.py:20
  48.9 1.3 dynamic-slice_select_fusion.3
  50.4 6.5 %collective-permute-start.6 = (f32[3,2,32,128]{3,2,1,0:T(8,128)S(1)}, f32[3,2,32,128]{3,2,1,0:T(8,128)S(1)}, u32[]{:S(2)}, u32[]{:S(2)}) collective-permute-start(f32[3,2,32,128]{3,2,1,0:T(8,128)S(1)} %get-tuple-element.66), channel_id=1, source_target_pairs={{16,0},{32,16},{48,32},{64,48},{80,64},{96,80},{112,96},{128,112},... | collective-permute-start | bytes 294920 | tf_op jit(solution)/shard_map/ppermute | solution.py:31
  56.9 1.9 collective-permute-start.5
  59.1 6.4 %collective-permute-done.5 = f32[3,2,32,128]{3,2,1,0:T(8,128)S(1)} collective-permute-done((f32[3,2,32,128]{3,2,1,0:T(8,128)S(1)}, f32[3,2,32,128]{3,2,1,0:T(8,128)S(1)}, u32[]{:S(2)}, u32[]{:S(2)}) %collective-permute-start.5) | collective-permute-done | bytes 98336 | tf_op jit(solution)/shard_map/ppermute | solution.py:28
  65.6 3.3 %collective-permute-start.8 = (f32[3,20,2,128]{3,2,1,0:T(2,128)S(1)}, f32[3,20,2,128]{3,2,1,0:T(2,128)S(1)}, u32[]{:S(2)}, u32[]{:S(2)}) collective-permute-start(f32[3,20,2,128]{3,2,1,0:T(2,128)S(1)} %get-tuple-element.58), channel_id=1, source_target_pairs={{1,0},{2,1},{3,2},{4,3},{5,4},{6,5},{7,6},{8,7},{9,8},{10,9},{11,1... | collective-permute-start | bytes 184328 | tf_op jit(solution)/shard_map/ppermute | solution.py:31
  68.8 1.9 collective-permute-start.7
  70.8 9.7 %collective-permute-done.7 = f32[3,20,2,128]{3,2,1,0:T(2,128)S(1)} collective-permute-done((f32[3,20,2,128]{3,2,1,0:T(2,128)S(1)}, f32[3,20,2,128]{3,2,1,0:T(2,128)S(1)}, u32[]{:S(2)}, u32[]{:S(2)}) %collective-permute-start.7) | collective-permute-done | bytes 61472 | tf_op jit(solution)/shard_map/ppermute | solution.py:28
  80.7 0.4 fusion.136
  81.1 0.4 fusion.137
  81.5 0.9 fusion.10
  83.6 0.6 fusion.38
  84.7 1.9 collective-permute-start.9
  87.9 0.6 slice_reduce_fusion.2
  91.1 8.6 %collective-permute-done.9 = f32[3,16,32,128]{3,2,1,0:T(8,128)} collective-permute-done((f32[3,16,32,128]{3,2,1,0:T(8,128)S(1)}, f32[3,16,32,128]{3,2,1,0:T(8,128)}, u32[]{:S(2)}, u32[]{:S(2)}) %collective-permute-start.9) | collective-permute-done | bytes 786464 | tf_op jit(solution)/shard_map/ppermute | solution.py:20
  99.7 1.3 dynamic-slice_select_fusion.2
  101.2 4.0 %collective-permute-start.11 = (f32[3,2,32,128]{3,2,1,0:T(8,128)S(1)}, f32[3,2,32,128]{3,2,1,0:T(8,128)S(1)}, u32[]{:S(2)}, u32[]{:S(2)}) collective-permute-start(f32[3,2,32,128]{3,2,1,0:T(8,128)S(1)} %get-tuple-element.64), channel_id=1, source_target_pairs={{16,0},{32,16},{48,32},{64,48},{80,64},{96,80},{112,96},{128,112},... | collective-permute-start | bytes 294920 | tf_op jit(solution)/shard_map/ppermute | solution.py:31
  105.3 1.9 collective-permute-start.10
  107.2 0.5 collective-permute-done.11
  107.7 6.1 %collective-permute-done.10 = f32[3,2,32,128]{3,2,1,0:T(8,128)S(1)} collective-permute-done((f32[3,2,32,128]{3,2,1,0:T(8,128)S(1)}, f32[3,2,32,128]{3,2,1,0:T(8,128)S(1)}, u32[]{:S(2)}, u32[]{:S(2)}) %collective-permute-start.10) | collective-permute-done | bytes 98336 | tf_op jit(solution)/shard_map/ppermute | solution.py:28
  113.9 1.9 collective-permute-start.13
  115.9 2.6 %collective-permute-start.12 = (f32[3,20,2,128]{3,2,1,0:T(2,128)S(1)}, f32[3,20,2,128]{3,2,1,0:T(2,128)S(1)}, u32[]{:S(2)}, u32[]{:S(2)}) collective-permute-start(f32[3,20,2,128]{3,2,1,0:T(2,128)S(1)} %get-tuple-element.55), channel_id=1, source_target_pairs={{0,1},{1,2},{2,3},{3,4},{4,5},{5,6},{6,7},{7,8},{8,9},{9,10},{10,1... | collective-permute-start | bytes 184328 | tf_op jit(solution)/shard_map/ppermute | solution.py:28
  118.5 9.4 %collective-permute-done.12 = f32[3,20,2,128]{3,2,1,0:T(2,128)S(1)} collective-permute-done((f32[3,20,2,128]{3,2,1,0:T(2,128)S(1)}, f32[3,20,2,128]{3,2,1,0:T(2,128)S(1)}, u32[]{:S(2)}, u32[]{:S(2)}) %collective-permute-start.12) | collective-permute-done | bytes 61472 | tf_op jit(solution)/shard_map/ppermute | solution.py:28
  128.1 0.4 fusion.134
  128.5 0.4 fusion.135
  128.9 0.9 fusion.5
  131.0 0.6 fusion.35
  132.1 1.9 collective-permute-start.14
  135.2 0.6 slice_reduce_fusion.1
  138.4 8.7 %collective-permute-done.14 = f32[3,16,32,128]{3,2,1,0:T(8,128)} collective-permute-done((f32[3,16,32,128]{3,2,1,0:T(8,128)S(1)}, f32[3,16,32,128]{3,2,1,0:T(8,128)}, u32[]{:S(2)}, u32[]{:S(2)}) %collective-permute-start.14) | collective-permute-done | bytes 786464 | tf_op jit(solution)/shard_map/ppermute | solution.py:20
  147.1 1.3 dynamic-slice_select_fusion.1
  148.6 4.0 %collective-permute-start.16 = (f32[3,2,32,128]{3,2,1,0:T(8,128)S(1)}, f32[3,2,32,128]{3,2,1,0:T(8,128)S(1)}, u32[]{:S(2)}, u32[]{:S(2)}) collective-permute-start(f32[3,2,32,128]{3,2,1,0:T(8,128)S(1)} %get-tuple-element.62), channel_id=1, source_target_pairs={{16,0},{32,16},{48,32},{64,48},{80,64},{96,80},{112,96},{128,112},... | collective-permute-start | bytes 294920 | tf_op jit(solution)/shard_map/ppermute | solution.py:31
  152.6 1.9 collective-permute-start.15
  154.5 0.6 collective-permute-done.16
  155.2 6.1 %collective-permute-done.15 = f32[3,2,32,128]{3,2,1,0:T(8,128)S(1)} collective-permute-done((f32[3,2,32,128]{3,2,1,0:T(8,128)S(1)}, f32[3,2,32,128]{3,2,1,0:T(8,128)S(1)}, u32[]{:S(2)}, u32[]{:S(2)}) %collective-permute-start.15) | collective-permute-done | bytes 98336 | tf_op jit(solution)/shard_map/ppermute | solution.py:28
  161.3 1.9 collective-permute-start.18
  163.2 2.4 %collective-permute-start.17 = (f32[3,20,2,128]{3,2,1,0:T(2,128)S(1)}, f32[3,20,2,128]{3,2,1,0:T(2,128)S(1)}, u32[]{:S(2)}, u32[]{:S(2)}) collective-permute-start(f32[3,20,2,128]{3,2,1,0:T(2,128)S(1)} %get-tuple-element.53), channel_id=1, source_target_pairs={{0,1},{1,2},{2,3},{3,4},{4,5},{5,6},{6,7},{7,8},{8,9},{9,10},{10,1... | collective-permute-start | bytes 184328 | tf_op jit(solution)/shard_map/ppermute | solution.py:28
  165.6 9.8 %collective-permute-done.17 = f32[3,20,2,128]{3,2,1,0:T(2,128)S(1)} collective-permute-done((f32[3,20,2,128]{3,2,1,0:T(2,128)S(1)}, f32[3,20,2,128]{3,2,1,0:T(2,128)S(1)}, u32[]{:S(2)}, u32[]{:S(2)}) %collective-permute-start.17) | collective-permute-done | bytes 61472 | tf_op jit(solution)/shard_map/ppermute | solution.py:28
  175.6 0.4 fusion.132
  176.0 0.4 fusion.133
  176.4 0.9 fusion
  178.5 0.6 fusion.32
  179.6 1.9 collective-permute-start.19
  182.6 0.6 slice_reduce_fusion
  185.8 7.8 %collective-permute-done.19 = f32[3,16,32,128]{3,2,1,0:T(8,128)} collective-permute-done((f32[3,16,32,128]{3,2,1,0:T(8,128)S(1)}, f32[3,16,32,128]{3,2,1,0:T(8,128)}, u32[]{:S(2)}, u32[]{:S(2)}) %collective-permute-start.19) | collective-permute-done | bytes 786464 | tf_op jit(solution)/shard_map/ppermute | solution.py:20
  193.6 1.3 dynamic-slice_select_fusion
  194.9 1.1 fusion.22
  (60 shorter events, 8.2 us)
Async XLA Ops:
  1.0 8.6 %collective-permute-start = (f32[3,2,32,128]{3,2,1,0:T(8,128)S(1)}, f32[3,2,32,128]{3,2,1,0:T(8,128)S(1)}, u32[]{:S(2)}, u32[]{:S(2)}) collective-permute-start(f32[3,2,32,128]{3,2,1,0:T(8,128)S(1)} %get-tuple-element.68), channel_id=1, source_target_pairs={{0,16},{16,32},{32,48},{48,64},{64,80},{80,96},{96,112},{112,128},... | collective-permute-start | bytes 294920 | tf_op jit(solution)/shard_map/ppermute | solution.py:28
  4.4 6.8 %collective-permute-start.1 = (f32[3,2,32,128]{3,2,1,0:T(8,128)S(1)}, f32[3,2,32,128]{3,2,1,0:T(8,128)S(1)}, u32[]{:S(2)}, u32[]{:S(2)}) collective-permute-start(f32[3,2,32,128]{3,2,1,0:T(8,128)S(1)} %get-tuple-element.67), channel_id=1, source_target_pairs={{16,0},{32,16},{48,32},{64,48},{80,64},{96,80},{112,96},{128,112},... | collective-permute-start | bytes 294920 | tf_op jit(solution)/shard_map/ppermute | solution.py:31
  11.2 6.1 %collective-permute-start.3 = (f32[3,20,2,128]{3,2,1,0:T(2,128)S(1)}, f32[3,20,2,128]{3,2,1,0:T(2,128)S(1)}, u32[]{:S(2)}, u32[]{:S(2)}) collective-permute-start(f32[3,20,2,128]{3,2,1,0:T(2,128)S(1)} %get-tuple-element.60), channel_id=1, source_target_pairs={{1,0},{2,1},{3,2},{4,3},{5,4},{6,5},{7,6},{8,7},{9,8},{10,9},{11,1... | collective-permute-start | bytes 184328 | tf_op jit(solution)/shard_map/ppermute | solution.py:31
  15.3 11.6 %collective-permute-start.2 = (f32[3,20,2,128]{3,2,1,0:T(2,128)S(1)}, f32[3,20,2,128]{3,2,1,0:T(2,128)S(1)}, u32[]{:S(2)}, u32[]{:S(2)}) collective-permute-start(f32[3,20,2,128]{3,2,1,0:T(2,128)S(1)} %get-tuple-element.59), channel_id=1, source_target_pairs={{0,1},{1,2},{2,3},{3,4},{4,5},{5,6},{6,7},{7,8},{8,9},{9,10},{10,1... | collective-permute-start | bytes 184328 | tf_op jit(solution)/shard_map/ppermute | solution.py:28
  30.9 7.1 %copy-start.1 = (s32[8]{0:T(128)S(1)}, s32[8]{0:T(128)}, u32[]{:S(2)}) copy-start(s32[8]{0:T(128)} %param.5) | copy-start | bytes 100
  31.0 11.6 %copy-start = (f32[3,16,32,128]{3,2,1,0:T(8,128)S(1)}, f32[3,16,32,128]{3,2,1,0:T(8,128)}, u32[]{:S(2)}) copy-start(f32[3,16,32,128]{3,2,1,0:T(8,128)} %param.4) | copy-start | bytes 2359300
  31.9 17.0 %collective-permute-start.4 = (f32[3,16,32,128]{3,2,1,0:T(8,128)}, f32[3,16,32,128]{3,2,1,0:T(8,128)}, u32[]{:S(2)}, u32[]{:S(2)}) collective-permute-start(f32[3,16,32,128]{3,2,1,0:T(8,128)} %pad_maximum_fusion.24), channel_id=1, source_target_pairs={{16,0},{32,16},{48,32},{64,48},{80,64},{96,80},{112,96},{128,112},... | collective-permute-start | bytes 2359304 | tf_op jit(solution)/shard_map/ppermute | solution.py:20
  50.4 8.7 %collective-permute-start.6 = (f32[3,2,32,128]{3,2,1,0:T(8,128)S(1)}, f32[3,2,32,128]{3,2,1,0:T(8,128)S(1)}, u32[]{:S(2)}, u32[]{:S(2)}) collective-permute-start(f32[3,2,32,128]{3,2,1,0:T(8,128)S(1)} %get-tuple-element.66), channel_id=1, source_target_pairs={{16,0},{32,16},{48,32},{64,48},{80,64},{96,80},{112,96},{128,112},... | collective-permute-start | bytes 294920 | tf_op jit(solution)/shard_map/ppermute | solution.py:31
  56.9 8.6 %collective-permute-start.5 = (f32[3,2,32,128]{3,2,1,0:T(8,128)S(1)}, f32[3,2,32,128]{3,2,1,0:T(8,128)S(1)}, u32[]{:S(2)}, u32[]{:S(2)}) collective-permute-start(f32[3,2,32,128]{3,2,1,0:T(8,128)S(1)} %get-tuple-element.65), channel_id=1, source_target_pairs={{0,16},{16,32},{32,48},{48,64},{64,80},{80,96},{96,112},{112,128},... | collective-permute-start | bytes 294920 | tf_op jit(solution)/shard_map/ppermute | solution.py:28
  65.6 5.2 %collective-permute-start.8 = (f32[3,20,2,128]{3,2,1,0:T(2,128)S(1)}, f32[3,20,2,128]{3,2,1,0:T(2,128)S(1)}, u32[]{:S(2)}, u32[]{:S(2)}) collective-permute-start(f32[3,20,2,128]{3,2,1,0:T(2,128)S(1)} %get-tuple-element.58), channel_id=1, source_target_pairs={{1,0},{2,1},{3,2},{4,3},{5,4},{6,5},{7,6},{8,7},{9,8},{10,9},{11,1... | collective-permute-start | bytes 184328 | tf_op jit(solution)/shard_map/ppermute | solution.py:31
  68.8 11.7 %collective-permute-start.7 = (f32[3,20,2,128]{3,2,1,0:T(2,128)S(1)}, f32[3,20,2,128]{3,2,1,0:T(2,128)S(1)}, u32[]{:S(2)}, u32[]{:S(2)}) collective-permute-start(f32[3,20,2,128]{3,2,1,0:T(2,128)S(1)} %get-tuple-element.57), channel_id=1, source_target_pairs={{0,1},{1,2},{2,3},{3,4},{4,5},{5,6},{6,7},{7,8},{8,9},{9,10},{10,1... | collective-permute-start | bytes 184328 | tf_op jit(solution)/shard_map/ppermute | solution.py:28
  84.7 15.0 %collective-permute-start.9 = (f32[3,16,32,128]{3,2,1,0:T(8,128)S(1)}, f32[3,16,32,128]{3,2,1,0:T(8,128)}, u32[]{:S(2)}, u32[]{:S(2)}) collective-permute-start(f32[3,16,32,128]{3,2,1,0:T(8,128)S(1)} %pad_maximum_fusion.25), channel_id=1, source_target_pairs={{16,0},{32,16},{48,32},{64,48},{80,64},{96,80},{112,96},{128,112},... | collective-permute-start | bytes 2359304 | tf_op jit(solution)/shard_map/ppermute | solution.py:20
  101.2 6.5 %collective-permute-start.11 = (f32[3,2,32,128]{3,2,1,0:T(8,128)S(1)}, f32[3,2,32,128]{3,2,1,0:T(8,128)S(1)}, u32[]{:S(2)}, u32[]{:S(2)}) collective-permute-start(f32[3,2,32,128]{3,2,1,0:T(8,128)S(1)} %get-tuple-element.64), channel_id=1, source_target_pairs={{16,0},{32,16},{48,32},{64,48},{80,64},{96,80},{112,96},{128,112},... | collective-permute-start | bytes 294920 | tf_op jit(solution)/shard_map/ppermute | solution.py:31
  105.3 8.6 %collective-permute-start.10 = (f32[3,2,32,128]{3,2,1,0:T(8,128)S(1)}, f32[3,2,32,128]{3,2,1,0:T(8,128)S(1)}, u32[]{:S(2)}, u32[]{:S(2)}) collective-permute-start(f32[3,2,32,128]{3,2,1,0:T(8,128)S(1)} %get-tuple-element.63), channel_id=1, source_target_pairs={{0,16},{16,32},{32,48},{48,64},{64,80},{80,96},{96,112},{112,128},... | collective-permute-start | bytes 294920 | tf_op jit(solution)/shard_map/ppermute | solution.py:28
  113.9 4.5 %collective-permute-start.13 = (f32[3,20,2,128]{3,2,1,0:T(2,128)S(1)}, f32[3,20,2,128]{3,2,1,0:T(2,128)S(1)}, u32[]{:S(2)}, u32[]{:S(2)}) collective-permute-start(f32[3,20,2,128]{3,2,1,0:T(2,128)S(1)} %get-tuple-element.56), channel_id=1, source_target_pairs={{1,0},{2,1},{3,2},{4,3},{5,4},{6,5},{7,6},{8,7},{9,8},{10,9},{11,1... | collective-permute-start | bytes 184328 | tf_op jit(solution)/shard_map/ppermute | solution.py:31
  115.9 12.0 %collective-permute-start.12 = (f32[3,20,2,128]{3,2,1,0:T(2,128)S(1)}, f32[3,20,2,128]{3,2,1,0:T(2,128)S(1)}, u32[]{:S(2)}, u32[]{:S(2)}) collective-permute-start(f32[3,20,2,128]{3,2,1,0:T(2,128)S(1)} %get-tuple-element.55), channel_id=1, source_target_pairs={{0,1},{1,2},{2,3},{3,4},{4,5},{5,6},{6,7},{7,8},{8,9},{9,10},{10,1... | collective-permute-start | bytes 184328 | tf_op jit(solution)/shard_map/ppermute | solution.py:28
  132.1 15.0 %collective-permute-start.14 = (f32[3,16,32,128]{3,2,1,0:T(8,128)S(1)}, f32[3,16,32,128]{3,2,1,0:T(8,128)}, u32[]{:S(2)}, u32[]{:S(2)}) collective-permute-start(f32[3,16,32,128]{3,2,1,0:T(8,128)S(1)} %pad_maximum_fusion.26), channel_id=1, source_target_pairs={{16,0},{32,16},{48,32},{64,48},{80,64},{96,80},{112,96},{128,112},... | collective-permute-start | bytes 2359304 | tf_op jit(solution)/shard_map/ppermute | solution.py:20
  148.6 6.5 %collective-permute-start.16 = (f32[3,2,32,128]{3,2,1,0:T(8,128)S(1)}, f32[3,2,32,128]{3,2,1,0:T(8,128)S(1)}, u32[]{:S(2)}, u32[]{:S(2)}) collective-permute-start(f32[3,2,32,128]{3,2,1,0:T(8,128)S(1)} %get-tuple-element.62), channel_id=1, source_target_pairs={{16,0},{32,16},{48,32},{64,48},{80,64},{96,80},{112,96},{128,112},... | collective-permute-start | bytes 294920 | tf_op jit(solution)/shard_map/ppermute | solution.py:31
  152.6 8.6 %collective-permute-start.15 = (f32[3,2,32,128]{3,2,1,0:T(8,128)S(1)}, f32[3,2,32,128]{3,2,1,0:T(8,128)S(1)}, u32[]{:S(2)}, u32[]{:S(2)}) collective-permute-start(f32[3,2,32,128]{3,2,1,0:T(8,128)S(1)} %get-tuple-element.61), channel_id=1, source_target_pairs={{0,16},{16,32},{32,48},{48,64},{64,80},{80,96},{96,112},{112,128},... | collective-permute-start | bytes 294920 | tf_op jit(solution)/shard_map/ppermute | solution.py:28
  161.3 4.3 %collective-permute-start.18 = (f32[3,20,2,128]{3,2,1,0:T(2,128)S(1)}, f32[3,20,2,128]{3,2,1,0:T(2,128)S(1)}, u32[]{:S(2)}, u32[]{:S(2)}) collective-permute-start(f32[3,20,2,128]{3,2,1,0:T(2,128)S(1)} %get-tuple-element.54), channel_id=1, source_target_pairs={{1,0},{2,1},{3,2},{4,3},{5,4},{6,5},{7,6},{8,7},{9,8},{10,9},{11,1... | collective-permute-start | bytes 184328 | tf_op jit(solution)/shard_map/ppermute | solution.py:31
  163.2 12.2 %collective-permute-start.17 = (f32[3,20,2,128]{3,2,1,0:T(2,128)S(1)}, f32[3,20,2,128]{3,2,1,0:T(2,128)S(1)}, u32[]{:S(2)}, u32[]{:S(2)}) collective-permute-start(f32[3,20,2,128]{3,2,1,0:T(2,128)S(1)} %get-tuple-element.53), channel_id=1, source_target_pairs={{0,1},{1,2},{2,3},{3,4},{4,5},{5,6},{6,7},{7,8},{8,9},{9,10},{10,1... | collective-permute-start | bytes 184328 | tf_op jit(solution)/shard_map/ppermute | solution.py:28
  179.6 14.0 %collective-permute-start.19 = (f32[3,16,32,128]{3,2,1,0:T(8,128)S(1)}, f32[3,16,32,128]{3,2,1,0:T(8,128)}, u32[]{:S(2)}, u32[]{:S(2)}) collective-permute-start(f32[3,16,32,128]{3,2,1,0:T(8,128)S(1)} %pad_maximum_fusion.27), channel_id=1, source_target_pairs={{16,0},{32,16},{48,32},{64,48},{80,64},{96,80},{112,96},{128,112},... | collective-permute-start | bytes 2359304 | tf_op jit(solution)/shard_map/ppermute | solution.py:20
where the time goes:
time: 197 us; the launch traced here: 196 us
  waiting for transfers between devices  90.9 us (46%)
  starting transfers between devices  60.1 us (31%)
  other arithmetic  20.7 us (11%)
  between operations  15.7 us (8%)
  local copies, waits for them, and re-layouts  8.47 us (4%)
    ppermute x8, waiting for transfers between devices, with_halo(): lax.ppermute(lax.slice_in_dim(block, block.shape[dim] - width, None, axis...  57.8 us
    ppermute x4, waiting for transfers between devices, passed_along(): lax.ppermute(value, axis, [(source, source + steps) for source in range(l...  31.4 us
    ppermute x8, starting transfers between devices, with_halo(): lax.ppermute(lax.slice_in_dim(block, 0, width, axis=dim), axis, backward)  30.3 us
    ppermute x8, starting transfers between devices, with_halo(): lax.ppermute(lax.slice_in_dim(block, block.shape[dim] - width, None, axis...  18 us
    ppermute x4, starting transfers between devices, passed_along(): lax.ppermute(value, axis, [(source, source + steps) for source in range(l...  11.9 us
    sub x8, other arithmetic, advance(): padded[:, 2:, 1:-1] + padded[:, :-2, 1:-1] + padded[:, 1:-1, 2:]  6.09 us
    slice x16, local copies, waits for them, and re-layouts, advance(): jnp.roll(centre, -1, 3)  5.45 us
    select_n x4, other arithmetic, slide_block(): incoming = jnp.where(at_end, melt_piece, received)  5.1 us
  transfers between devices with their start and end apart: 20, of which 16 were waited for; matrix products, arithmetic and copies ran while one was open for 2% of the time, Pallas kernels for 0%

commit v1 on v0

v1 whole, which is shorter than its diff:
```python
import functools

import jax
import jax.numpy as jnp
from jax import lax
from jax.experimental import pallas as pl
from jax.experimental.pallas import tpu as pltpu
from jax.sharding import PartitionSpec as P

MESH = pl.DeviceIdType.MESH
STEPS = 8
OWN = 16
FAR = 8
PLANES = OWN + OWN + FAR
COLS = 32
LO = 16
ROWS = 64
CHUNK = 2
NEAR_CHUNKS = OWN // CHUNK
FAR_CHUNKS = FAR // CHUNK
CHUNKS = NEAR_CHUNKS + FAR_CHUNKS
LAG = 2


def kernel(G, W, slide, fields, melt, out, lev, mbuf, cur, local_sem, x_send, x_recv, y_send, y_recv, m_send, m_recv):
    g = lax.axis_index("grow")
    w = lax.axis_index("wide")
    base = OWN * (G - g)
    has_left, has_right = w > 0, w < W - 1
    partners = (
        (g > 0, {"grow": g - 1}), (g < G - 1, {"grow": g + 1}),
        (g > 1, {"grow": g - 2}), (g < G - 2, {"grow": g + 2}),
        (has_left, {"wide": w - 1}), (has_right, {"wide": w + 1}),
    )
    barrier = pltpu.get_barrier_semaphore()
    count = jnp.int32(0)
    for there, device in partners:
        count = count + there.astype(jnp.int32)

        @pl.when(there)
        def _():
            pl.semaphore_signal(barrier, inc=1, device_id=device, device_id_type=MESH)

    own = pltpu.make_async_copy(fields, lev.at[0, :, pl.ds(0, OWN), pl.ds(LO, COLS), :], local_sem.at[0])
    own.start()
    melt_in = pltpu.make_async_copy(melt, mbuf.at[:, :, pl.ds(LO, COLS), :], local_sem.at[1])

    @pl.when(g >= G - 2)
    def _():
        melt_in.start()

    cursor = jnp.int32(0)
    cur[0] = cursor
    for k in range(STEPS):
        cursor = cursor + slide[k]
        cur[k + 1] = cursor

    zeros = jnp.zeros((8, 128), jnp.float32)
    for side_there, row in ((has_left, LO - 8), (has_right, LO + COLS)):

        @pl.when(jnp.logical_not(side_there))
        def _():
            @pl.loop(0, PLANES)
            def _(x):
                for f in range(3):
                    lev[0, f, x, pl.ds(row, 8), :] = zeros

            @pl.loop(0, OWN)
            def _(x):
                for f in range(3):
                    mbuf[f, x, pl.ds(row, 8), :] = zeros

    def zero_planes(first, last):
        @pl.loop(first, last)
        def _(x):
            for f in range(3):
                for k in range(6):
                    lev[0, f, x, pl.ds(LO - 8 + 8 * k, 8), :] = zeros

    @pl.when(g == G - 1)
    def _():
        zero_planes(OWN, PLANES)

    @pl.when(g == G - 2)
    def _():
        zero_planes(2 * OWN, PLANES)

    def x_copy(c):
        return pltpu.make_async_remote_copy(
            src_ref=fields.at[:, pl.ds(CHUNK * c, CHUNK)],
            dst_ref=lev.at[0, :, pl.ds(OWN + CHUNK * c, CHUNK), pl.ds(LO, COLS), :],
            send_sem=x_send.at[c], recv_sem=x_recv.at[c], device_id={"grow": g - 1}, device_id_type=MESH)

    def far_copy(c):
        return pltpu.make_async_remote_copy(
            src_ref=fields.at[:, pl.ds(CHUNK * c, CHUNK)],
            dst_ref=lev.at[0, :, pl.ds(2 * OWN + CHUNK * c, CHUNK), pl.ds(LO, COLS), :],
            send_sem=x_send.at[NEAR_CHUNKS + c], recv_sem=x_recv.at[NEAR_CHUNKS + c],
            device_id={"grow": g - 2}, device_id_type=MESH)

    def y_own(side):
        rows, to, there = ((0, LO + COLS, w - 1), (COLS - 8, LO - 8, w + 1))[side]
        return pltpu.make_async_remote_copy(
            src_ref=fields.at[:, :, pl.ds(rows, 8), :],
            dst_ref=lev.at[0, :, pl.ds(0, OWN), pl.ds(to, 8), :],
            send_sem=y_send.at[side, CHUNKS], recv_sem=y_recv.at[side, CHUNKS],
            device_id={"wide": there}, device_id_type=MESH)

    def y_melt(side):
        rows, to, there = ((0, LO + COLS, w - 1), (COLS - 8, LO - 8, w + 1))[side]
        return pltpu.make_async_remote_copy(
            src_ref=melt.at[:, :, pl.ds(rows, 8), :],
            dst_ref=mbuf.at[:, :, pl.ds(to, 8), :],
            send_sem=m_send.at[side], recv_sem=m_recv.at[side],
            device_id={"wide": there}, device_id_type=MESH)

    def y_copy(side, c):
        rows, to, there = ((LO, LO + COLS, w - 1), (LO + COLS - 8, LO - 8, w + 1))[side]
        x = OWN + CHUNK * c
        return pltpu.make_async_remote_copy(
            src_ref=lev.at[0, :, pl.ds(x, CHUNK), pl.ds(rows, 8), :],
            dst_ref=lev.at[0, :, pl.ds(x, CHUNK), pl.ds(to, 8), :],
            send_sem=y_send.at[side, c], recv_sem=y_recv.at[side, c],
            device_id={"wide": there}, device_id_type=MESH)

    sends = (has_left, has_right)
    receives = (has_right, has_left)

    pl.semaphore_wait(barrier, count)
    for side in (0, 1):
        @pl.when(sends[side])
        def _():
            y_own(side).start()

    @pl.when(g > 0)
    def _():
        @pl.loop(0, NEAR_CHUNKS)
        def _(c):
            x_copy(c).start()

    @pl.when(g > 1)
    def _():
        @pl.loop(0, FAR_CHUNKS)
        def _(c):
            far_copy(c).start()

    @pl.when(g >= G - 2)
    def _():
        for side in (0, 1):
            @pl.when(sends[side])
            def _():
                y_melt(side).start()

    def pair(t, x):
        for k in range(6):
            row = LO - 8 + 8 * k
            total, centre = [[], []], [[], []]
            for f in range(3):
                along = [lev[t, f, x + d, pl.ds(row, 8), :] for d in (-1, 0, 1, 2)]
                for q in range(2):
                    here = along[q + 1]
                    around = along[q] + along[q + 2]
                    around = around + lev[t, f, x + q, pl.ds(row - 1, 8), :] + lev[t, f, x + q, pl.ds(row + 1, 8), :]
                    around = around + (pltpu.roll(here, 1, 1) + pltpu.roll(here, 127, 1))
                    total[q].append(around)
                    centre[q].append(here)
            for q in range(2):
                p, s, h = centre[q]
                p2 = p * p
                rest = 1.0 - p2
                drive = p * (0.4 - 0.3 * p2) + 0.15 * total[q][0] - rest * rest * (0.4 * h + 0.6 * s)
                grown = jnp.tanh(drive)
                change = 0.5 * (grown - p)
                s = (0.4 * s + 0.1 * total[q][1]) + change
                h = (0.04 * h + 0.16 * total[q][2]) + change
                new = [grown, s, h]
                if k == 0:
                    new = [jnp.where(has_left, v, 0.0) for v in new]
                if k == 5:
                    new = [jnp.where(has_right, v, 0.0) for v in new]
                for f in range(3):
                    lev[t + 1, f, x + q, pl.ds(row, 8), :] = new[f]

    span = pl.ds(LO - 8, COLS + 16)

    def left_edge(t, x):
        @pl.when(jnp.logical_and(g == 0, x < OWN))
        def _():
            for q in range(2):
                keep = x + q >= cur[t + 1]
                for f in range(3):
                    lev[t + 1, f, x + q, span, :] = jnp.where(keep, lev[t + 1, f, x + q, span, :], 0.0)

    def right_edge(t, x):
        for q in range(2):
            @pl.when(x + q >= base)
            def _():
                plane = x + q - base
                inside = cur[t] > plane
                enters = cur[t + 1] > plane
                slot = jnp.minimum(plane, OWN - 1)
                for f in range(3):
                    fresh = jnp.where(enters, mbuf[f, slot, span, :], 0.0)
                    lev[t + 1, f, x + q, span, :] = jnp.where(inside, lev[t + 1, f, x + q, span, :], fresh)

    own.wait()
    for side in (0, 1):
        @pl.when(receives[side])
        def _():
            y_own(side).wait_recv()

    @pl.when(g >= G - 2)
    def _():
        melt_in.wait()
        for side in (0, 1):
            @pl.when(receives[side])
            def _():
                y_melt(side).wait_recv()

    @pl.loop(0, STEPS - 1)
    def _(t):
        @pl.loop(0, OWN // 2 - 1 - t)
        def _(i):
            x = t + 1 + 2 * i
            pair(t, x)
            left_edge(t, x)

    def pass_on(c):
        for side in (0, 1):
            @pl.when(sends[side])
            def _():
                y_copy(side, c).start()

    def edges_in(c):
        for side in (0, 1):
            @pl.when(receives[side])
            def _():
                y_copy(side, c).wait_recv()

    @pl.loop(0, NEAR_CHUNKS + LAG)
    def _(it):
        @pl.when(jnp.logical_and(it < NEAR_CHUNKS, g < G - 1))
        def _():
            x_copy(it).wait_recv()
            pass_on(it)

            @pl.when(jnp.logical_and(it % 2 == 1, g < G - 2))
            def _():
                far_copy(it // 2).wait_recv()
                pass_on(NEAR_CHUNKS + it // 2)

        @pl.when(it >= LAG)
        def _():
            c = it - LAG

            @pl.when(g < G - 1)
            def _():
                edges_in(c)

            @pl.loop(0, STEPS)
            def _(t):
                x = OWN + CHUNK * c - 1 - t
                pair(t, x)
                left_edge(t, x)
                right_edge(t, x)

    @pl.when(g < G - 2)
    def _():
        @pl.loop(NEAR_CHUNKS, CHUNKS)
        def _(c):
            edges_in(c)

    @pl.loop(0, STEPS)
    def _(t):
        @pl.loop(0, FAR // 2)
        def _(i):
            x = 2 * OWN - 1 - t + 2 * i
            pair(t, x)
            right_edge(t, x)

    shift = cur[STEPS]
    @pl.loop(0, OWN)
    def _(x):
        for f in range(3):
            out[f, x] = lev[STEPS, f, shift + x, pl.ds(LO, COLS), :]

    for side in (0, 1):
        @pl.when(sends[side])
        def _():
            y_own(side).wait_send()

            @pl.when(g >= G - 2)
            def _():
                y_melt(side).wait_send()

            @pl.when(g < G - 1)
            def _():
                @pl.loop(0, NEAR_CHUNKS)
                def _(c):
                    y_copy(side, c).wait_send()

            @pl.when(g < G - 2)
            def _():
                @pl.loop(NEAR_CHUNKS, CHUNKS)
                def _(c):
                    y_copy(side, c).wait_send()

    @pl.when(g > 0)
    def _():
        @pl.loop(0, NEAR_CHUNKS)
        def _(c):
            x_copy(c).wait_send()

    @pl.when(g > 1)
    def _():
        @pl.loop(0, FAR_CHUNKS)
        def _(c):
            far_copy(c).wait_send()


def solution(mesh):
    G, W = mesh.shape["grow"], mesh.shape["wide"]

    def body(fields, melt_planes, slide_planes):
        dma = pltpu.SemaphoreType.DMA
        return pl.pallas_call(
            functools.partial(kernel, G, W),
            out_shape=jax.ShapeDtypeStruct(fields.shape, jnp.float32),
            in_specs=[
                pl.BlockSpec(memory_space=pltpu.SMEM),
                pl.BlockSpec(memory_space=pl.ANY),
                pl.BlockSpec(memory_space=pl.ANY),
            ],
            out_specs=pl.BlockSpec(memory_space=pltpu.VMEM),
            scratch_shapes=[
                pltpu.VMEM((STEPS + 1, 3, PLANES, ROWS, 128), jnp.float32),
                pltpu.VMEM((3, OWN, ROWS, 128), jnp.float32),
                pltpu.SMEM((STEPS + 1,), jnp.int32),
                dma((2,)), dma((CHUNKS,)), dma((CHUNKS,)),
                dma((2, CHUNKS + 1)), dma((2, CHUNKS + 1)), dma((2,)), dma((2,)),
            ],
            compiler_params=pltpu.CompilerParams(
                collective_id=0, has_side_effects=True, vmem_limit_bytes=60 * 1024 * 1024),
        )(slide_planes, fields, melt_planes)

    return jax.shard_map(
        body, mesh=mesh,
        in_specs=(P(None, "grow", "wide", None), P(None, None, "wide", None), P()),
        out_specs=P(None, "grow", "wide", None), check_vma=False)
```

time: 197 us -> 72 us (0.37)
  the two profiles are of different devices: /device:TPU:224 before, /device:TPU:57 now
where the time goes in v1:
time: 72 us; the launch traced here: 71.9 us
  Pallas kernels  69.8 us (97%)
  local copies, waits for them, and re-layouts  2.06 us (3%)
    pallas_call x1, Pallas kernels, body(): pl.pallas_call(functools.partial(kernel, G, W), out_shape=jax.ShapeDtypeS...  69.8 us
    unnamed x1, local copies, waits for them, and re-layouts  2.06 us

profile of v1, /device:TPU:57, one launch (start us, length us, event | category | flops | bytes accessed | tf_op | source)
XLA Modules:
  0.0 71.9 jit_solution(6706758008157929572)
XLA Ops:
  0.0 69.8 %shard_map.37 = f32[3,16,32,128]{3,2,1,0:T(8,128)} custom-call(s32[8]{0:T(128)} %slide.1, f32[3,16,32,128]{3,2,1,0:T(8,128)} %fields.1, f32[3,16,32,128]{3,2,1,0:T(8,128)} %melt.1), custom_call_target="tpu_custom_call" | custom-call | tf_op jit(solution)/shard_map/pallas_call | solution.py:326
  69.8 2.1 %copy.5 = f32[3,16,32,128]{3,2,1,0:T(8,128)} copy(f32[3,16,32,128]{3,2,1,0:T(8,128)} %shard_map.37) | data formatting | bytes 1572864

commit v2 on v1

v2 whole, which is shorter than its diff:
```python
import functools

import jax
import jax.numpy as jnp
from jax import lax
from jax.experimental import pallas as pl
from jax.experimental.pallas import tpu as pltpu
from jax.sharding import PartitionSpec as P

MESH = pl.DeviceIdType.MESH
STEPS = 8
OWN = 16
FAR = 8
PLANES = OWN + OWN + FAR
COLS = 32
LO = 16
ROWS = 64
PAD = 2
CHUNK = 2
NEAR_CHUNKS = OWN // CHUNK
FAR_CHUNK = 4
FAR_CHUNKS = FAR // FAR_CHUNK
CHUNKS = NEAR_CHUNKS + FAR_CHUNKS
GROUP = 4
RING = 4


def kernel(G, W, slide, fields, melt, out, lev, mbuf, rbuf, cur, local_sem,
           x_send, x_recv, r_send, r_recv, y_send, y_recv, m_send, m_recv):
    g = lax.axis_index("grow")
    w = lax.axis_index("wide")
    base = OWN * (G - g)
    has_left, has_right = w > 0, w < W - 1
    start, place = g - g % RING, g % RING
    relay_to = start + (place + 1) % RING
    relay_from = start + (place + RING - 1) % RING
    source = g + 2
    far_from = source - source % RING + (source + 1) % RING
    relays = relay_from > 1
    partners = (
        (g > 0, {"grow": g - 1}), (g < G - 1, {"grow": g + 1}),
        (g > 1, {"grow": relay_to}), (relays, {"grow": relay_from}),
        (relays, {"grow": relay_from - 2}), (g < G - 2, {"grow": far_from}),
        (has_left, {"wide": w - 1}), (has_right, {"wide": w + 1}),
    )
    barrier = pltpu.get_barrier_semaphore()
    count = jnp.int32(0)
    for there, device in partners:
        count = count + there.astype(jnp.int32)

        @pl.when(there)
        def _():
            pl.semaphore_signal(barrier, inc=1, device_id=device, device_id_type=MESH)

    own = pltpu.make_async_copy(fields, lev.at[0, :, pl.ds(PAD + 0, OWN), pl.ds(LO, COLS), :], local_sem.at[0])
    own.start()
    melt_in = pltpu.make_async_copy(melt, mbuf.at[:, :, pl.ds(LO, COLS), :], local_sem.at[1])

    @pl.when(g >= G - 2)
    def _():
        melt_in.start()

    cursor = jnp.int32(0)
    cur[0] = cursor
    for k in range(STEPS):
        cursor = cursor + slide[k]
        cur[k + 1] = cursor

    zeros = jnp.zeros((8, 128), jnp.float32)
    for side_there, row in ((has_left, LO - 8), (has_right, LO + COLS)):

        @pl.when(jnp.logical_not(side_there))
        def _():
            @pl.loop(0, PLANES)
            def _(x):
                for f in range(3):
                    lev[0, f, PAD + x, pl.ds(row, 8), :] = zeros

            @pl.loop(0, OWN)
            def _(x):
                for f in range(3):
                    mbuf[f, x, pl.ds(row, 8), :] = zeros

    def zero_planes(first, last):
        @pl.loop(first, last)
        def _(x):
            for f in range(3):
                for k in range(6):
                    lev[0, f, PAD + x, pl.ds(LO - 8 + 8 * k, 8), :] = zeros

    @pl.when(g == G - 1)
    def _():
        zero_planes(OWN, PLANES)

    @pl.when(g == G - 2)
    def _():
        zero_planes(2 * OWN, PLANES)

    def x_copy(c):
        return pltpu.make_async_remote_copy(
            src_ref=fields.at[:, pl.ds(CHUNK * c, CHUNK)],
            dst_ref=lev.at[0, :, pl.ds(PAD + OWN + CHUNK * c, CHUNK), pl.ds(LO, COLS), :],
            send_sem=x_send.at[c], recv_sem=x_recv.at[c], device_id={"grow": g - 1}, device_id_type=MESH)

    def relay_copy(c):
        return pltpu.make_async_remote_copy(
            src_ref=fields.at[:, pl.ds(FAR_CHUNK * c, FAR_CHUNK)],
            dst_ref=rbuf.at[:, pl.ds(FAR_CHUNK * c, FAR_CHUNK)],
            send_sem=r_send.at[c], recv_sem=r_recv.at[c], device_id={"grow": relay_to}, device_id_type=MESH)

    def far_copy(c):
        return pltpu.make_async_remote_copy(
            src_ref=rbuf.at[:, pl.ds(FAR_CHUNK * c, FAR_CHUNK)],
            dst_ref=lev.at[0, :, pl.ds(PAD + 2 * OWN + FAR_CHUNK * c, FAR_CHUNK), pl.ds(LO, COLS), :],
            send_sem=x_send.at[NEAR_CHUNKS + c], recv_sem=x_recv.at[NEAR_CHUNKS + c],
            device_id={"grow": relay_from - 2}, device_id_type=MESH)

    def y_own(side):
        rows, to, there = ((0, LO + COLS, w - 1), (COLS - 8, LO - 8, w + 1))[side]
        return pltpu.make_async_remote_copy(
            src_ref=fields.at[:, :, pl.ds(rows, 8), :],
            dst_ref=lev.at[0, :, pl.ds(PAD + 0, OWN), pl.ds(to, 8), :],
            send_sem=y_send.at[side, CHUNKS], recv_sem=y_recv.at[side, CHUNKS],
            device_id={"wide": there}, device_id_type=MESH)

    def y_melt(side):
        rows, to, there = ((0, LO + COLS, w - 1), (COLS - 8, LO - 8, w + 1))[side]
        return pltpu.make_async_remote_copy(
            src_ref=melt.at[:, :, pl.ds(rows, 8), :],
            dst_ref=mbuf.at[:, :, pl.ds(to, 8), :],
            send_sem=m_send.at[side], recv_sem=m_recv.at[side],
            device_id={"wide": there}, device_id_type=MESH)

    def y_copy(side, c, far=False):
        rows, to, there = ((LO, LO + COLS, w - 1), (LO + COLS - 8, LO - 8, w + 1))[side]
        size = FAR_CHUNK if far else CHUNK
        x = (2 * OWN if far else OWN) + size * c
        slot = NEAR_CHUNKS + c if far else c
        return pltpu.make_async_remote_copy(
            src_ref=lev.at[0, :, pl.ds(PAD + x, size), pl.ds(rows, 8), :],
            dst_ref=lev.at[0, :, pl.ds(PAD + x, size), pl.ds(to, 8), :],
            send_sem=y_send.at[side, slot], recv_sem=y_recv.at[side, slot],
            device_id={"wide": there}, device_id_type=MESH)

    sends = (has_left, has_right)
    receives = (has_right, has_left)

    pl.semaphore_wait(barrier, count)
    for side in (0, 1):
        @pl.when(sends[side])
        def _():
            y_own(side).start()

    @pl.when(g > 0)
    def _():
        @pl.loop(0, NEAR_CHUNKS)
        def _(c):
            x_copy(c).start()

    @pl.when(g > 1)
    def _():
        @pl.loop(0, FAR_CHUNKS)
        def _(c):
            relay_copy(c).start()

    @pl.when(g >= G - 2)
    def _():
        for side in (0, 1):
            @pl.when(sends[side])
            def _():
                y_melt(side).start()

    def advance(t, x):
        for k in range(6):
            row = LO - 8 + 8 * k
            total, centre = [[] for _ in range(GROUP)], [[] for _ in range(GROUP)]
            for f in range(3):
                along = [lev[t, f, PAD + x + d, pl.ds(row, 8), :] for d in range(-1, GROUP + 1)]
                for q in range(GROUP):
                    here = along[q + 1]
                    around = along[q] + along[q + 2]
                    around = around + lev[t, f, PAD + x + q, pl.ds(row - 1, 8), :] + lev[t, f, PAD + x + q, pl.ds(row + 1, 8), :]
                    around = around + (pltpu.roll(here, 1, 1) + pltpu.roll(here, 127, 1))
                    total[q].append(around)
                    centre[q].append(here)
            for q in range(GROUP):
                p, s, h = centre[q]
                p2 = p * p
                rest = 1.0 - p2
                drive = p * (0.4 - 0.3 * p2) + 0.15 * total[q][0] - rest * rest * (0.4 * h + 0.6 * s)
                grown = jnp.tanh(drive)
                change = 0.5 * (grown - p)
                s = (0.4 * s + 0.1 * total[q][1]) + change
                h = (0.04 * h + 0.16 * total[q][2]) + change
                new = [grown, s, h]
                if k == 0:
                    new = [jnp.where(has_left, v, 0.0) for v in new]
                if k == 5:
                    new = [jnp.where(has_right, v, 0.0) for v in new]
                for f in range(3):
                    lev[t + 1, f, PAD + x + q, pl.ds(row, 8), :] = new[f]

    span = pl.ds(LO - 8, COLS + 16)

    def left_edge(t, x):
        @pl.when(jnp.logical_and(g == 0, x < OWN))
        def _():
            for q in range(GROUP):
                keep = x + q >= cur[t + 1]
                for f in range(3):
                    lev[t + 1, f, PAD + x + q, span, :] = jnp.where(keep, lev[t + 1, f, PAD + x + q, span, :], 0.0)

    def right_edge(t, x):
        for q in range(GROUP):
            @pl.when(x + q >= base)
            def _():
                plane = x + q - base
                inside = cur[t] > plane
                enters = cur[t + 1] > plane
                slot = jnp.minimum(plane, OWN - 1)
                for f in range(3):
                    fresh = jnp.where(enters, mbuf[f, slot, span, :], 0.0)
                    lev[t + 1, f, PAD + x + q, span, :] = jnp.where(inside, lev[t + 1, f, PAD + x + q, span, :], fresh)

    own.wait()
    for side in (0, 1):
        @pl.when(receives[side])
        def _():
            y_own(side).wait_recv()

    @pl.when(g >= G - 2)
    def _():
        melt_in.wait()
        for side in (0, 1):
            @pl.when(receives[side])
            def _():
                y_melt(side).wait_recv()

    @pl.loop(0, STEPS - 1)
    def _(t):
        groups = (OWN - 2 - 2 * t + GROUP - 1) // GROUP

        @pl.loop(0, groups)
        def _(i):
            x = OWN - 1 - t - GROUP * (groups - i)
            advance(t, x)
            left_edge(t, x)

    def pass_on(c, far=False):
        for side in (0, 1):
            @pl.when(sends[side])
            def _():
                y_copy(side, c, far).start()

    def edges_in(c, far=False):
        for side in (0, 1):
            @pl.when(receives[side])
            def _():
                y_copy(side, c, far).wait_recv()

    def arrive(c):
        @pl.when(g < G - 1)
        def _():
            x_copy(c).wait_recv()
            pass_on(c)

    groups = OWN // GROUP
    arrive(0)

    @pl.loop(0, groups)
    def _(j):
        arrive(2 * j + 1)

        @pl.when(jnp.logical_and(j < FAR_CHUNKS, relays))
        def _():
            relay_copy(j).wait_recv()
            far_copy(j).start()

        @pl.when(jnp.logical_and(j >= groups - FAR_CHUNKS, g < G - 2))
        def _():
            c = j - (groups - FAR_CHUNKS)
            far_copy(c).wait_recv()
            pass_on(c, True)

        @pl.when(j < groups - 1)
        def _():
            arrive(2 * j + 2)

        @pl.when(g < G - 1)
        def _():
            edges_in(2 * j)
            edges_in(2 * j + 1)

        @pl.loop(0, STEPS)
        def _(t):
            x = OWN + GROUP * j - 1 - t
            advance(t, x)
            left_edge(t, x)
            right_edge(t, x)

    @pl.when(g < G - 2)
    def _():
        for c in range(FAR_CHUNKS):
            edges_in(c, True)

    @pl.loop(0, STEPS)
    def _(t):
        @pl.loop(0, FAR // GROUP)
        def _(i):
            x = 2 * OWN - 1 - t + GROUP * i
            advance(t, x)
            right_edge(t, x)

    shift = cur[STEPS]
    @pl.loop(0, OWN)
    def _(x):
        for f in range(3):
            out[f, x] = lev[STEPS, f, PAD + shift + x, pl.ds(LO, COLS), :]

    for side in (0, 1):
        @pl.when(sends[side])
        def _():
            y_own(side).wait_send()

            @pl.when(g >= G - 2)
            def _():
                y_melt(side).wait_send()

            @pl.when(g < G - 1)
            def _():
                @pl.loop(0, NEAR_CHUNKS)
                def _(c):
                    y_copy(side, c).wait_send()

            @pl.when(g < G - 2)
            def _():
                for c in range(FAR_CHUNKS):
                    y_copy(side, c, True).wait_send()

    @pl.when(g > 0)
    def _():
        @pl.loop(0, NEAR_CHUNKS)
        def _(c):
            x_copy(c).wait_send()

    for c in range(FAR_CHUNKS):
        @pl.when(g > 1)
        def _():
            relay_copy(c).wait_send()

        @pl.when(relays)
        def _():
            far_copy(c).wait_send()


def solution(mesh):
    G, W = mesh.shape["grow"], mesh.shape["wide"]

    def body(fields, melt_planes, slide_planes):
        dma = pltpu.SemaphoreType.DMA
        return pl.pallas_call(
            functools.partial(kernel, G, W),
            out_shape=jax.ShapeDtypeStruct(fields.shape, jnp.float32),
            in_specs=[
                pl.BlockSpec(memory_space=pltpu.SMEM),
                pl.BlockSpec(memory_space=pl.ANY),
                pl.BlockSpec(memory_space=pl.ANY),
            ],
            out_specs=pl.BlockSpec(memory_space=pltpu.VMEM),
            scratch_shapes=[
                pltpu.VMEM((STEPS + 1, 3, PAD + PLANES, ROWS, 128), jnp.float32),
                pltpu.VMEM((3, OWN, ROWS, 128), jnp.float32),
                pltpu.VMEM((3, FAR, COLS, 128), jnp.float32),
                pltpu.SMEM((STEPS + 1,), jnp.int32),
                dma((2,)), dma((CHUNKS,)), dma((CHUNKS,)), dma((FAR_CHUNKS,)), dma((FAR_CHUNKS,)),
                dma((2, CHUNKS + 1)), dma((2, CHUNKS + 1)), dma((2,)), dma((2,)),
            ],
            compiler_params=pltpu.CompilerParams(
                collective_id=0, has_side_effects=True, vmem_limit_bytes=60 * 1024 * 1024),
        )(slide_planes, fields, melt_planes)

    return jax.shard_map(
        body, mesh=mesh,
        in_specs=(P(None, "grow", "wide", None), P(None, None, "wide", None), P()),
        out_specs=P(None, "grow", "wide", None), check_vma=False)
```

time: 72 us -> 63.3 us (0.88)
  Pallas kernels: 69.8 us -> 61.1 us
    pallas_call x1, Pallas kernels: 69.8 us -> 61.1 us  [body(): pl.pallas_call(functools.partial(kernel, G, W), out_shape=jax.ShapeDtypeS...]
where the time goes in v2:
time: 63.3 us; the launch traced here: 63.2 us
  Pallas kernels  61.1 us (97%)
  local copies, waits for them, and re-layouts  2.06 us (3%)
    pallas_call x1, Pallas kernels, body(): pl.pallas_call(functools.partial(kernel, G, W), out_shape=jax.ShapeDtypeS...  61.1 us
    unnamed x1, local copies, waits for them, and re-layouts  2.06 us

profile of v2, /device:TPU:57, one launch (start us, length us, event | category | flops | bytes accessed | tf_op | source)
XLA Modules:
  0.0 63.2 jit_solution(3603079418817042438)
XLA Ops:
  0.0 61.1 %shard_map.37 = f32[3,16,32,128]{3,2,1,0:T(8,128)} custom-call(s32[8]{0:T(128)} %slide.1, f32[3,16,32,128]{3,2,1,0:T(8,128)} %fields.1, f32[3,16,32,128]{3,2,1,0:T(8,128)} %melt.1), custom_call_target="tpu_custom_call" | custom-call | tf_op jit(solution)/shard_map/pallas_call | solution.py:361
  61.1 2.1 %copy.5 = f32[3,16,32,128]{3,2,1,0:T(8,128)} copy(f32[3,16,32,128]{3,2,1,0:T(8,128)} %shard_map.37) | data formatting | bytes 1572864

commit v3 on v2

--- a/solution.py
+++ b/solution.py
@@ -265,11 +265,16 @@
             pass_on(c)
 
     groups = OWN // GROUP
-    arrive(0)
+    middle = jnp.logical_or(w == W // 2 - 1, w == W // 2)
+    ahead = jnp.where(middle, 5, 3)
 
     @pl.loop(0, groups)
     def _(j):
-        arrive(2 * j + 1)
+        first = jnp.where(j == 0, 0, jnp.minimum(2 * j - 2 + ahead, NEAR_CHUNKS))
+
+        @pl.loop(first, jnp.minimum(2 * j + ahead, NEAR_CHUNKS))
+        def _(c):
+            arrive(c)
 
         @pl.when(jnp.logical_and(j < FAR_CHUNKS, relays))
         def _():
@@ -281,10 +286,6 @@
             c = j - (groups - FAR_CHUNKS)
             far_copy(c).wait_recv()
             pass_on(c, True)
-
-        @pl.when(j < groups - 1)
-        def _():
-            arrive(2 * j + 2)
 
         @pl.when(g < G - 1)
         def _():

time: 63.3 us -> 57.3 us (0.905)
  Pallas kernels: 61.1 us -> 55 us
    pallas_call x1, Pallas kernels: 61.1 us -> 55 us  [body(): pl.pallas_call(functools.partial(kernel, G, W), out_shape=jax.ShapeDtypeS...]
where the time goes in v3:
time: 57.3 us; the launch traced here: 57.1 us
  Pallas kernels  55 us (96%)
  local copies, waits for them, and re-layouts  2.06 us (4%)
    pallas_call x1, Pallas kernels, body(): pl.pallas_call(functools.partial(kernel, G, W), out_shape=jax.ShapeDtypeS...  55 us
    unnamed x1, local copies, waits for them, and re-layouts  2.06 us

profile of v3, /device:TPU:57, one launch (start us, length us, event | category | flops | bytes accessed | tf_op | source)
XLA Modules:
  0.0 57.1 jit_solution(1946951448030087915)
XLA Ops:
  0.0 55.0 %shard_map.37 = f32[3,16,32,128]{3,2,1,0:T(8,128)} custom-call(s32[8]{0:T(128)} %slide.1, f32[3,16,32,128]{3,2,1,0:T(8,128)} %fields.1, f32[3,16,32,128]{3,2,1,0:T(8,128)} %melt.1), custom_call_target="tpu_custom_call" | custom-call | tf_op jit(solution)/shard_map/pallas_call | solution.py:362
  55.0 2.1 %copy.5 = f32[3,16,32,128]{3,2,1,0:T(8,128)} copy(f32[3,16,32,128]{3,2,1,0:T(8,128)} %shard_map.37) | data formatting | bytes 1572864

commit v4 on v3

--- a/solution.py
+++ b/solution.py
@@ -23,10 +23,11 @@
 CHUNKS = NEAR_CHUNKS + FAR_CHUNKS
 GROUP = 4
 RING = 4
-
-
-def kernel(G, W, slide, fields, melt, out, lev, mbuf, rbuf, cur, local_sem,
-           x_send, x_recv, r_send, r_recv, y_send, y_recv, m_send, m_recv):
+EARLY = 5
+
+
+def kernel(G, W, slide, fields, melt, out, lev, mbuf, rbuf, ebuf, cur, local_sem,
+           x_send, x_recv, r_send, r_recv, y_send, y_recv, m_send, m_recv, e_send, e_recv):
     g = lax.axis_index("grow")
     w = lax.axis_index("wide")
     base = OWN * (G - g)
@@ -115,6 +116,28 @@
             send_sem=x_send.at[NEAR_CHUNKS + c], recv_sem=x_recv.at[NEAR_CHUNKS + c],
             device_id={"grow": relay_from - 2}, device_id_type=MESH)
 
+    middle = (w == W // 2 - 1, w == W // 2)
+    edge_rows = (LO + COLS, LO - 8)
+
+    def near_edge(side):
+        rows = pl.ds(edge_rows[side], 8)
+        return pltpu.make_async_remote_copy(
+            src_ref=lev.at[0, :, pl.ds(PAD, OWN), rows, :],
+            dst_ref=lev.at[0, :, pl.ds(PAD + OWN, OWN), rows, :],
+            send_sem=e_send.at[0], recv_sem=e_recv.at[0], device_id={"grow": g - 1}, device_id_type=MESH)
+
+    def relay_edge(side):
+        return pltpu.make_async_remote_copy(
+            src_ref=lev.at[0, :, pl.ds(PAD, FAR), pl.ds(edge_rows[side], 8), :],
+            dst_ref=ebuf,
+            send_sem=e_send.at[1], recv_sem=e_recv.at[1], device_id={"grow": relay_to}, device_id_type=MESH)
+
+    def far_edge(side):
+        return pltpu.make_async_remote_copy(
+            src_ref=ebuf,
+            dst_ref=lev.at[0, :, pl.ds(PAD + 2 * OWN, FAR), pl.ds(edge_rows[side], 8), :],
+            send_sem=e_send.at[2], recv_sem=e_recv.at[2], device_id={"grow": relay_from - 2}, device_id_type=MESH)
+
     def y_own(side):
         rows, to, there = ((0, LO + COLS, w - 1), (COLS - 8, LO - 8, w + 1))[side]
         return pltpu.make_async_remote_copy(
@@ -144,6 +167,8 @@
 
     sends = (has_left, has_right)
     receives = (has_right, has_left)
+    passes = (jnp.logical_and(has_left, w != W // 2), jnp.logical_and(has_right, w != W // 2 - 1))
+    gets = (jnp.logical_and(has_right, w != W // 2 - 1), jnp.logical_and(has_left, w != W // 2))
 
     pl.semaphore_wait(barrier, count)
     for side in (0, 1):
@@ -153,7 +178,7 @@
 
     @pl.when(g > 0)
     def _():
-        @pl.loop(0, NEAR_CHUNKS)
+        @pl.loop(0, jnp.where(jnp.logical_or(*middle), EARLY, NEAR_CHUNKS))
         def _(c):
             x_copy(c).start()
 
@@ -228,6 +253,19 @@
         def _():
             y_own(side).wait_recv()
 
+    for side in (0, 1):
+        @pl.when(jnp.logical_and(middle[side], g > 0))
+        def _():
+            near_edge(side).start()
+
+            @pl.loop(EARLY, NEAR_CHUNKS)
+            def _(c):
+                x_copy(c).start()
+
+        @pl.when(jnp.logical_and(middle[side], g > 1))
+        def _():
+            relay_edge(side).start()
+
     @pl.when(g >= G - 2)
     def _():
         melt_in.wait()
@@ -248,13 +286,13 @@
 
     def pass_on(c, far=False):
         for side in (0, 1):
-            @pl.when(sends[side])
+            @pl.when(passes[side])
             def _():
                 y_copy(side, c, far).start()
 
     def edges_in(c, far=False):
         for side in (0, 1):
-            @pl.when(receives[side])
+            @pl.when(gets[side])
             def _():
                 y_copy(side, c, far).wait_recv()
 
@@ -265,8 +303,7 @@
             pass_on(c)
 
     groups = OWN // GROUP
-    middle = jnp.logical_or(w == W // 2 - 1, w == W // 2)
-    ahead = jnp.where(middle, 5, 3)
+    ahead = 3
 
     @pl.loop(0, groups)
     def _(j):
@@ -286,6 +323,16 @@
             c = j - (groups - FAR_CHUNKS)
             far_copy(c).wait_recv()
             pass_on(c, True)
+
+        for side in (0, 1):
+            @pl.when(jnp.logical_and(jnp.logical_and(middle[side], relays), j == 2))
+            def _():
+                relay_edge(side).wait_recv()
+                far_edge(side).start()
+
+            @pl.when(jnp.logical_and(jnp.logical_and(middle[side], g < G - 1), j == 0))
+            def _():
+                near_edge(side).wait_recv()
 
         @pl.when(g < G - 1)
         def _():
@@ -303,6 +350,11 @@
     def _():
         for c in range(FAR_CHUNKS):
             edges_in(c, True)
+
+        for side in (0, 1):
+            @pl.when(middle[side])
+            def _():
+                far_edge(side).wait_recv()
 
     @pl.loop(0, STEPS)
     def _(t):
@@ -327,16 +379,28 @@
             def _():
                 y_melt(side).wait_send()
 
-            @pl.when(g < G - 1)
-            def _():
-                @pl.loop(0, NEAR_CHUNKS)
-                def _(c):
-                    y_copy(side, c).wait_send()
-
-            @pl.when(g < G - 2)
-            def _():
-                for c in range(FAR_CHUNKS):
-                    y_copy(side, c, True).wait_send()
+        @pl.when(jnp.logical_and(passes[side], g < G - 1))
+        def _():
+            @pl.loop(0, NEAR_CHUNKS)
+            def _(c):
+                y_copy(side, c).wait_send()
+
+        @pl.when(jnp.logical_and(passes[side], g < G - 2))
+        def _():
+            for c in range(FAR_CHUNKS):
+                y_copy(side, c, True).wait_send()
+
+        @pl.when(jnp.logical_and(middle[side], g > 0))
+        def _():
+            near_edge(side).wait_send()
+
+        @pl.when(jnp.logical_and(middle[side], g > 1))
+        def _():
+            relay_edge(side).wait_send()
+
+        @pl.when(jnp.logical_and(middle[side], relays))
+        def _():
+            far_edge(side).wait_send()
 
     @pl.when(g > 0)
     def _():
@@ -372,9 +436,10 @@
                 pltpu.VMEM((STEPS + 1, 3, PAD + PLANES, ROWS, 128), jnp.float32),
                 pltpu.VMEM((3, OWN, ROWS, 128), jnp.float32),
                 pltpu.VMEM((3, FAR, COLS, 128), jnp.float32),
+                pltpu.VMEM((3, FAR, 8, 128), jnp.float32),
                 pltpu.SMEM((STEPS + 1,), jnp.int32),
                 dma((2,)), dma((CHUNKS,)), dma((CHUNKS,)), dma((FAR_CHUNKS,)), dma((FAR_CHUNKS,)),
-                dma((2, CHUNKS + 1)), dma((2, CHUNKS + 1)), dma((2,)), dma((2,)),
+                dma((2, CHUNKS + 1)), dma((2, CHUNKS + 1)), dma((2,)), dma((2,)), dma((3,)), dma((3,)),
             ],
             compiler_params=pltpu.CompilerParams(
                 collective_id=0, has_side_effects=True, vmem_limit_bytes=60 * 1024 * 1024),

time: 57.3 us -> 48.9 us (0.85)
  the two profiles are of different devices: /device:TPU:57 before, /device:TPU:30 now
where the time goes in v4:
time: 48.9 us; the launch traced here: 48.8 us
  Pallas kernels  46.7 us (96%)
  local copies, waits for them, and re-layouts  2.06 us (4%)
    pallas_call x1, Pallas kernels, body(): pl.pallas_call(functools.partial(kernel, G, W), out_shape=jax.ShapeDtypeS...  46.7 us
    unnamed x1, local copies, waits for them, and re-layouts  2.06 us

profile of v4, /device:TPU:30, one launch (start us, length us, event | category | flops | bytes accessed | tf_op | source)
XLA Modules:
  0.0 48.8 jit_solution(1538584925158849846)
XLA Ops:
  0.0 46.7 %shard_map.37 = f32[3,16,32,128]{3,2,1,0:T(8,128)} custom-call(s32[8]{0:T(128)} %slide.1, f32[3,16,32,128]{3,2,1,0:T(8,128)} %fields.1, f32[3,16,32,128]{3,2,1,0:T(8,128)} %melt.1), custom_call_target="tpu_custom_call" | custom-call | tf_op jit(solution)/shard_map/pallas_call | solution.py:426
  46.7 2.1 %copy.5 = f32[3,16,32,128]{3,2,1,0:T(8,128)} copy(f32[3,16,32,128]{3,2,1,0:T(8,128)} %shard_map.37) | data formatting | bytes 1572864

commit v5 on v4

--- a/solution.py
+++ b/solution.py
@@ -21,9 +21,8 @@
 FAR_CHUNK = 4
 FAR_CHUNKS = FAR // FAR_CHUNK
 CHUNKS = NEAR_CHUNKS + FAR_CHUNKS
-GROUP = 4
 RING = 4
-EARLY = 5
+EARLY = 6
 
 
 def kernel(G, W, slide, fields, melt, out, lev, mbuf, rbuf, ebuf, cur, local_sem,
@@ -195,20 +194,20 @@
             def _():
                 y_melt(side).start()
 
-    def advance(t, x):
+    def advance(t, x, n):
         for k in range(6):
             row = LO - 8 + 8 * k
-            total, centre = [[] for _ in range(GROUP)], [[] for _ in range(GROUP)]
+            total, centre = [[] for _ in range(n)], [[] for _ in range(n)]
             for f in range(3):
-                along = [lev[t, f, PAD + x + d, pl.ds(row, 8), :] for d in range(-1, GROUP + 1)]
-                for q in range(GROUP):
+                along = [lev[t, f, PAD + x + d, pl.ds(row, 8), :] for d in range(-1, n + 1)]
+                for q in range(n):
                     here = along[q + 1]
                     around = along[q] + along[q + 2]
                     around = around + lev[t, f, PAD + x + q, pl.ds(row - 1, 8), :] + lev[t, f, PAD + x + q, pl.ds(row + 1, 8), :]
                     around = around + (pltpu.roll(here, 1, 1) + pltpu.roll(here, 127, 1))
                     total[q].append(around)
                     centre[q].append(here)
-            for q in range(GROUP):
+            for q in range(n):
                 p, s, h = centre[q]
                 p2 = p * p
                 rest = 1.0 - p2
@@ -227,27 +226,87 @@
 
     span = pl.ds(LO - 8, COLS + 16)
 
-    def left_edge(t, x):
+    def left_edge(t, x, n):
         @pl.when(jnp.logical_and(g == 0, x < OWN))
         def _():
-            for q in range(GROUP):
+            for q in range(n):
                 keep = x + q >= cur[t + 1]
                 for f in range(3):
                     lev[t + 1, f, PAD + x + q, span, :] = jnp.where(keep, lev[t + 1, f, PAD + x + q, span, :], 0.0)
 
-    def right_edge(t, x):
-        for q in range(GROUP):
-            @pl.when(x + q >= base)
-            def _():
+    def right_edge(t, x, n):
+        @pl.when(x + n > base)
+        def _():
+            before, after = cur[t], cur[t + 1]
+            for q in range(n):
                 plane = x + q - base
-                inside = cur[t] > plane
-                enters = cur[t + 1] > plane
-                slot = jnp.minimum(plane, OWN - 1)
+                slot = jnp.clip(plane, 0, OWN - 1)
+                inside = before > plane
+                enters = after > plane
                 for f in range(3):
                     fresh = jnp.where(enters, mbuf[f, slot, span, :], 0.0)
                     lev[t + 1, f, PAD + x + q, span, :] = jnp.where(inside, lev[t + 1, f, PAD + x + q, span, :], fresh)
 
+    def pass_on(c, far=False):
+        for side in (0, 1):
+            @pl.when(passes[side])
+            def _():
+                y_copy(side, c, far).start()
+
+    def edges_in(c, far=False):
+        for side in (0, 1):
+            @pl.when(gets[side])
+            def _():
+                y_copy(side, c, far).wait_recv()
+
+    def arrive(first, last):
+        @pl.when(g < G - 1)
+        def _():
+            @pl.loop(first, last)
+            def _(c):
+                x_copy(c).wait_recv()
+                pass_on(c)
+
+    def arrive_far(c):
+        @pl.when(g < G - 2)
+        def _():
+            far_copy(c).wait_recv()
+            pass_on(c, True)
+
+    def hand_over(c):
+        @pl.when(relays)
+        def _():
+            relay_copy(c).wait_recv()
+            far_copy(c).start()
+
+    def edges(first, last):
+        @pl.when(g < G - 1)
+        def _():
+            @pl.loop(first, last)
+            def _(c):
+                edges_in(c)
+
+    def wave(first, n):
+        @pl.loop(0, STEPS)
+        def _(t):
+            x = first - 1 - t
+            advance(t, x, n)
+            if first <= OWN + STEPS:
+                left_edge(t, x, n)
+            right_edge(t, x, n)
+
+    def start_of_stream():
+        arrive(0, 2)
+        hand_over(0)
+        arrive(2, 4)
+
+    in_middle = jnp.logical_or(*middle)
     own.wait()
+
+    @pl.when(in_middle)
+    def _():
+        start_of_stream()
+
     for side in (0, 1):
         @pl.when(receives[side])
         def _():
@@ -276,75 +335,40 @@
 
     @pl.loop(0, STEPS - 1)
     def _(t):
-        groups = (OWN - 2 - 2 * t + GROUP - 1) // GROUP
+        groups = (OWN - 2 - 2 * t + 3) // 4
 
         @pl.loop(0, groups)
         def _(i):
-            x = OWN - 1 - t - GROUP * (groups - i)
-            advance(t, x)
-            left_edge(t, x)
-
-    def pass_on(c, far=False):
-        for side in (0, 1):
-            @pl.when(passes[side])
-            def _():
-                y_copy(side, c, far).start()
-
-    def edges_in(c, far=False):
-        for side in (0, 1):
-            @pl.when(gets[side])
-            def _():
-                y_copy(side, c, far).wait_recv()
-
-    def arrive(c):
-        @pl.when(g < G - 1)
-        def _():
-            x_copy(c).wait_recv()
-            pass_on(c)
-
-    groups = OWN // GROUP
-    ahead = 3
-
-    @pl.loop(0, groups)
-    def _(j):
-        first = jnp.where(j == 0, 0, jnp.minimum(2 * j - 2 + ahead, NEAR_CHUNKS))
-
-        @pl.loop(first, jnp.minimum(2 * j + ahead, NEAR_CHUNKS))
-        def _(c):
-            arrive(c)
-
-        @pl.when(jnp.logical_and(j < FAR_CHUNKS, relays))
-        def _():
-            relay_copy(j).wait_recv()
-            far_copy(j).start()
-
-        @pl.when(jnp.logical_and(j >= groups - FAR_CHUNKS, g < G - 2))
-        def _():
-            c = j - (groups - FAR_CHUNKS)
-            far_copy(c).wait_recv()
-            pass_on(c, True)
-
-        for side in (0, 1):
-            @pl.when(jnp.logical_and(jnp.logical_and(middle[side], relays), j == 2))
-            def _():
-                relay_edge(side).wait_recv()
-                far_edge(side).start()
-
-            @pl.when(jnp.logical_and(jnp.logical_and(middle[side], g < G - 1), j == 0))
-            def _():
-                near_edge(side).wait_recv()
-
-        @pl.when(g < G - 1)
-        def _():
-            edges_in(2 * j)
-            edges_in(2 * j + 1)
-
-        @pl.loop(0, STEPS)
-        def _(t):
-            x = OWN + GROUP * j - 1 - t
-            advance(t, x)
-            left_edge(t, x)
-            right_edge(t, x)
+            x = OWN - 1 - t - 4 * (groups - i)
+            advance(t, x, 4)
+            left_edge(t, x, 4)
+
+    @pl.when(jnp.logical_not(in_middle))
+    def _():
+        start_of_stream()
+
+    hand_over(1)
+    arrive(4, 5)
+    for side in (0, 1):
+        @pl.when(jnp.logical_and(middle[side], relays))
+        def _():
+            relay_edge(side).wait_recv()
+            far_edge(side).start()
+
+        @pl.when(jnp.logical_and(middle[side], g < G - 1))
+        def _():
+            near_edge(side).wait_recv()
+
+    edges(0, 4)
+    wave(OWN, 8)
+    arrive(5, 7)
+    arrive_far(0)
+    edges(4, 6)
+    wave(OWN + 8, 4)
+    arrive(7, 8)
+    arrive_far(1)
+    edges(6, 8)
+    wave(OWN + 12, 4)
 
     @pl.when(g < G - 2)
     def _():
@@ -356,13 +380,7 @@
             def _():
                 far_edge(side).wait_recv()
 
-    @pl.loop(0, STEPS)
-    def _(t):
-        @pl.loop(0, FAR // GROUP)
-        def _(i):
-            x = 2 * OWN - 1 - t + GROUP * i
-            advance(t, x)
-            right_edge(t, x)
+    wave(2 * OWN, 8)
 
     shift = cur[STEPS]
     @pl.loop(0, OWN)

time: 48.9 us -> 58.4 us (1.19)
  the two profiles are of different devices: /device:TPU:30 before, /device:TPU:17 now
where the time goes in v5:
time: 58.4 us; the launch traced here: 58.2 us
  Pallas kernels  56.1 us (96%)
  local copies, waits for them, and re-layouts  2.06 us (4%)
    pallas_call x1, Pallas kernels, body(): pl.pallas_call(functools.partial(kernel, G, W), out_shape=jax.ShapeDtypeS...  56.1 us
    unnamed x1, local copies, waits for them, and re-layouts  2.06 us

profile of v5, /device:TPU:17, one launch (start us, length us, event | category | flops | bytes accessed | tf_op | source)
XLA Modules:
  0.0 58.2 jit_solution(9528529887163743956)
XLA Ops:
  0.0 56.1 %shard_map.37 = f32[3,16,32,128]{3,2,1,0:T(8,128)} custom-call(s32[8]{0:T(128)} %slide.1, f32[3,16,32,128]{3,2,1,0:T(8,128)} %fields.1, f32[3,16,32,128]{3,2,1,0:T(8,128)} %melt.1), custom_call_target="tpu_custom_call" | custom-call | tf_op jit(solution)/shard_map/pallas_call | solution.py:444
  56.1 2.1 %copy.5 = f32[3,16,32,128]{3,2,1,0:T(8,128)} copy(f32[3,16,32,128]{3,2,1,0:T(8,128)} %shard_map.37) | data formatting | bytes 1572864

commit v6 on v5

--- a/solution.py
+++ b/solution.py
@@ -16,17 +16,13 @@
 LO = 16
 ROWS = 64
 PAD = 2
-CHUNK = 2
-NEAR_CHUNKS = OWN // CHUNK
-FAR_CHUNK = 4
-FAR_CHUNKS = FAR // FAR_CHUNK
-CHUNKS = NEAR_CHUNKS + FAR_CHUNKS
+HALF = 8
+QUAD = 4
 RING = 4
-EARLY = 6
 
 
 def kernel(G, W, slide, fields, melt, out, lev, mbuf, rbuf, ebuf, cur, local_sem,
-           x_send, x_recv, r_send, r_recv, y_send, y_recv, m_send, m_recv, e_send, e_recv):
+           n_send, n_recv, r_send, r_recv, f_send, f_recv, y_send, y_recv, m_send, m_recv, e_send, e_recv):
     g = lax.axis_index("grow")
     w = lax.axis_index("wide")
     base = OWN * (G - g)
@@ -96,53 +92,54 @@
     def _():
         zero_planes(2 * OWN, PLANES)
 
-    def x_copy(c):
+    def remote(src, dst, sems, index, device):
         return pltpu.make_async_remote_copy(
-            src_ref=fields.at[:, pl.ds(CHUNK * c, CHUNK)],
-            dst_ref=lev.at[0, :, pl.ds(PAD + OWN + CHUNK * c, CHUNK), pl.ds(LO, COLS), :],
-            send_sem=x_send.at[c], recv_sem=x_recv.at[c], device_id={"grow": g - 1}, device_id_type=MESH)
-
-    def relay_copy(c):
-        return pltpu.make_async_remote_copy(
-            src_ref=fields.at[:, pl.ds(FAR_CHUNK * c, FAR_CHUNK)],
-            dst_ref=rbuf.at[:, pl.ds(FAR_CHUNK * c, FAR_CHUNK)],
-            send_sem=r_send.at[c], recv_sem=r_recv.at[c], device_id={"grow": relay_to}, device_id_type=MESH)
-
-    def far_copy(c):
-        return pltpu.make_async_remote_copy(
-            src_ref=rbuf.at[:, pl.ds(FAR_CHUNK * c, FAR_CHUNK)],
-            dst_ref=lev.at[0, :, pl.ds(PAD + 2 * OWN + FAR_CHUNK * c, FAR_CHUNK), pl.ds(LO, COLS), :],
-            send_sem=x_send.at[NEAR_CHUNKS + c], recv_sem=x_recv.at[NEAR_CHUNKS + c],
-            device_id={"grow": relay_from - 2}, device_id_type=MESH)
+            src_ref=src, dst_ref=dst, send_sem=sems[0].at[index], recv_sem=sems[1].at[index],
+            device_id=device, device_id_type=MESH)
+
+    def near(part):
+        if part < 4:
+            first, planes, row, rows = HALF * (part // 2), HALF, (COLS - 8) * (part % 2), 8
+        else:
+            first, planes, row, rows = QUAD * (part - 4), QUAD, 8, COLS - 16
+        return remote(fields.at[:, pl.ds(first, planes), pl.ds(row, rows), :],
+                      lev.at[0, :, pl.ds(PAD + OWN + first, planes), pl.ds(LO + row, rows), :],
+                      (n_send, n_recv), part, {"grow": g - 1})
+
+    far_rows = ((0, 8), (COLS - 8, 8), (8, COLS - 16))
+
+    def relay(part):
+        rows = pl.ds(*far_rows[part])
+        return remote(fields.at[:, pl.ds(0, FAR), rows, :], rbuf.at[:, :, rows, :],
+                      (r_send, r_recv), part, {"grow": relay_to})
+
+    def far(part):
+        row, rows = far_rows[part]
+        return remote(rbuf.at[:, :, pl.ds(row, rows), :],
+                      lev.at[0, :, pl.ds(PAD + 2 * OWN, FAR), pl.ds(LO + row, rows), :],
+                      (f_send, f_recv), part, {"grow": relay_from - 2})
 
     middle = (w == W // 2 - 1, w == W // 2)
-    edge_rows = (LO + COLS, LO - 8)
-
-    def near_edge(side):
-        rows = pl.ds(edge_rows[side], 8)
-        return pltpu.make_async_remote_copy(
-            src_ref=lev.at[0, :, pl.ds(PAD, OWN), rows, :],
-            dst_ref=lev.at[0, :, pl.ds(PAD + OWN, OWN), rows, :],
-            send_sem=e_send.at[0], recv_sem=e_recv.at[0], device_id={"grow": g - 1}, device_id_type=MESH)
-
-    def relay_edge(side):
-        return pltpu.make_async_remote_copy(
-            src_ref=lev.at[0, :, pl.ds(PAD, FAR), pl.ds(edge_rows[side], 8), :],
-            dst_ref=ebuf,
-            send_sem=e_send.at[1], recv_sem=e_recv.at[1], device_id={"grow": relay_to}, device_id_type=MESH)
-
-    def far_edge(side):
-        return pltpu.make_async_remote_copy(
-            src_ref=ebuf,
-            dst_ref=lev.at[0, :, pl.ds(PAD + 2 * OWN, FAR), pl.ds(edge_rows[side], 8), :],
-            send_sem=e_send.at[2], recv_sem=e_recv.at[2], device_id={"grow": relay_from - 2}, device_id_type=MESH)
+    in_middle = jnp.logical_or(*middle)
+
+    def halo(first, planes, side):
+        return lev.at[0, :, pl.ds(PAD + first, planes), pl.ds((LO + COLS, LO - 8)[side], 8), :]
+
+    def near_halo(side):
+        return remote(halo(0, OWN, side), halo(OWN, OWN, side), (e_send, e_recv), 0, {"grow": g - 1})
+
+    def relay_halo(side):
+        return remote(halo(0, FAR, side), ebuf, (e_send, e_recv), 1, {"grow": relay_to})
+
+    def far_halo(side):
+        return remote(ebuf, halo(2 * OWN, FAR, side), (e_send, e_recv), 2, {"grow": relay_from - 2})
 
     def y_own(side):
         rows, to, there = ((0, LO + COLS, w - 1), (COLS - 8, LO - 8, w + 1))[side]
         return pltpu.make_async_remote_copy(
             src_ref=fields.at[:, :, pl.ds(rows, 8), :],
             dst_ref=lev.at[0, :, pl.ds(PAD + 0, OWN), pl.ds(to, 8), :],
-            send_sem=y_send.at[side, CHUNKS], recv_sem=y_recv.at[side, CHUNKS],
+            send_sem=y_send.at[side, 3], recv_sem=y_recv.at[side, 3],
             device_id={"wide": there}, device_id_type=MESH)
 
     def y_melt(side):
@@ -153,16 +150,11 @@
             send_sem=m_send.at[side], recv_sem=m_recv.at[side],
             device_id={"wide": there}, device_id_type=MESH)
 
-    def y_copy(side, c, far=False):
-        rows, to, there = ((LO, LO + COLS, w - 1), (LO + COLS - 8, LO - 8, w + 1))[side]
-        size = FAR_CHUNK if far else CHUNK
-        x = (2 * OWN if far else OWN) + size * c
-        slot = NEAR_CHUNKS + c if far else c
-        return pltpu.make_async_remote_copy(
-            src_ref=lev.at[0, :, pl.ds(PAD + x, size), pl.ds(rows, 8), :],
-            dst_ref=lev.at[0, :, pl.ds(PAD + x, size), pl.ds(to, 8), :],
-            send_sem=y_send.at[side, slot], recv_sem=y_recv.at[side, slot],
-            device_id={"wide": there}, device_id_type=MESH)
+    def y_copy(side, c):
+        row, to, there = ((LO, LO + COLS, w - 1), (LO + COLS - 8, LO - 8, w + 1))[side]
+        planes = pl.ds(PAD + OWN + HALF * c, HALF)
+        return remote(lev.at[0, :, planes, pl.ds(row, 8), :], lev.at[0, :, planes, pl.ds(to, 8), :],
+                      (y_send.at[side], y_recv.at[side]), c, {"wide": there})
 
     sends = (has_left, has_right)
     receives = (has_right, has_left)
@@ -177,15 +169,18 @@
 
     @pl.when(g > 0)
     def _():
-        @pl.loop(0, jnp.where(jnp.logical_or(*middle), EARLY, NEAR_CHUNKS))
-        def _(c):
-            x_copy(c).start()
+        for part in range(6):
+            near(part).start()
+
+        @pl.when(jnp.logical_not(in_middle))
+        def _():
+            for part in range(6, 8):
+                near(part).start()
 
     @pl.when(g > 1)
     def _():
-        @pl.loop(0, FAR_CHUNKS)
-        def _(c):
-            relay_copy(c).start()
+        for part in range(3):
+            relay(part).start()
 
     @pl.when(g >= G - 2)
     def _():
@@ -247,66 +242,42 @@
                     fresh = jnp.where(enters, mbuf[f, slot, span, :], 0.0)
                     lev[t + 1, f, PAD + x + q, span, :] = jnp.where(inside, lev[t + 1, f, PAD + x + q, span, :], fresh)
 
-    def pass_on(c, far=False):
+    def pass_on(c, copies):
         for side in (0, 1):
+            copies[side].wait_recv()
+
             @pl.when(passes[side])
             def _():
-                y_copy(side, c, far).start()
-
-    def edges_in(c, far=False):
+                y_copy(side, c).start()
+
+    def near_edges(half):
+        @pl.when(g < G - 1)
+        def _():
+            pass_on(half, (near(2 * half), near(2 * half + 1)))
+
+    def far_edges():
+        @pl.when(g < G - 2)
+        def _():
+            pass_on(2, (far(0), far(1)))
+
+    def hand_over(*parts):
+        @pl.when(relays)
+        def _():
+            for part in parts:
+                relay(part).wait_recv()
+                far(part).start()
+
+    def edges_in(c):
         for side in (0, 1):
             @pl.when(gets[side])
             def _():
-                y_copy(side, c, far).wait_recv()
-
-    def arrive(first, last):
-        @pl.when(g < G - 1)
-        def _():
-            @pl.loop(first, last)
-            def _(c):
-                x_copy(c).wait_recv()
-                pass_on(c)
-
-    def arrive_far(c):
-        @pl.when(g < G - 2)
-        def _():
-            far_copy(c).wait_recv()
-            pass_on(c, True)
-
-    def hand_over(c):
-        @pl.when(relays)
-        def _():
-            relay_copy(c).wait_recv()
-            far_copy(c).start()
-
-    def edges(first, last):
-        @pl.when(g < G - 1)
-        def _():
-            @pl.loop(first, last)
-            def _(c):
-                edges_in(c)
-
-    def wave(first, n):
-        @pl.loop(0, STEPS)
-        def _(t):
-            x = first - 1 - t
-            advance(t, x, n)
-            if first <= OWN + STEPS:
-                left_edge(t, x, n)
-            right_edge(t, x, n)
-
-    def start_of_stream():
-        arrive(0, 2)
-        hand_over(0)
-        arrive(2, 4)
-
-    in_middle = jnp.logical_or(*middle)
+                y_copy(side, c).wait_recv()
+
+    near_edges(0)
+    hand_over(0, 1)
+    near_edges(1)
+
     own.wait()
-
-    @pl.when(in_middle)
-    def _():
-        start_of_stream()
-
     for side in (0, 1):
         @pl.when(receives[side])
         def _():
@@ -315,15 +286,18 @@
     for side in (0, 1):
         @pl.when(jnp.logical_and(middle[side], g > 0))
         def _():
-            near_edge(side).start()
-
-            @pl.loop(EARLY, NEAR_CHUNKS)
-            def _(c):
-                x_copy(c).start()
+            near_halo(side).start()
+            for part in range(6, 8):
+                near(part).start()
 
         @pl.when(jnp.logical_and(middle[side], g > 1))
         def _():
-            relay_edge(side).start()
+            relay_halo(side).start()
+
+    @pl.when(in_middle)
+    def _():
+        hand_over(2)
+        far_edges()
 
     @pl.when(g >= G - 2)
     def _():
@@ -345,42 +319,52 @@
 
     @pl.when(jnp.logical_not(in_middle))
     def _():
-        start_of_stream()
-
-    hand_over(1)
-    arrive(4, 5)
+        hand_over(2)
+
     for side in (0, 1):
         @pl.when(jnp.logical_and(middle[side], relays))
         def _():
-            relay_edge(side).wait_recv()
-            far_edge(side).start()
-
-        @pl.when(jnp.logical_and(middle[side], g < G - 1))
-        def _():
-            near_edge(side).wait_recv()
-
-    edges(0, 4)
-    wave(OWN, 8)
-    arrive(5, 7)
-    arrive_far(0)
-    edges(4, 6)
-    wave(OWN + 8, 4)
-    arrive(7, 8)
-    arrive_far(1)
-    edges(6, 8)
-    wave(OWN + 12, 4)
-
-    @pl.when(g < G - 2)
-    def _():
-        for c in range(FAR_CHUNKS):
-            edges_in(c, True)
+            relay_halo(side).wait_recv()
+            far_halo(side).start()
+
+    @pl.loop(0, 5)
+    def _(stage):
+        for k in range(4):
+            @pl.when(jnp.logical_and(stage == k, g < G - 1))
+            def _():
+                near(4 + k).wait_recv()
+                if k % 2 == 0:
+                    edges_in(k // 2)
+
+        @pl.when(jnp.logical_and(stage == 0, jnp.logical_not(in_middle)))
+        def _():
+            far_edges()
 
         for side in (0, 1):
-            @pl.when(middle[side])
-            def _():
-                far_edge(side).wait_recv()
-
-    wave(2 * OWN, 8)
+            @pl.when(jnp.logical_and(jnp.logical_and(stage == 0, g < G - 1), middle[side]))
+            def _():
+                near_halo(side).wait_recv()
+
+        @pl.when(jnp.logical_and(stage == 4, g < G - 2))
+        def _():
+            far(2).wait_recv()
+            edges_in(2)
+            for side in (0, 1):
+                @pl.when(middle[side])
+                def _():
+                    far_halo(side).wait_recv()
+
+        first = OWN + QUAD * stage
+        parts = jnp.where(stage == 4, 2, 1)
+
+        @pl.loop(0, STEPS)
+        def _(t):
+            @pl.loop(0, parts)
+            def _(i):
+                x = first - 1 - t + QUAD * i
+                advance(t, x, QUAD)
+                left_edge(t, x, QUAD)
+                right_edge(t, x, QUAD)
 
     shift = cur[STEPS]
     @pl.loop(0, OWN)
@@ -399,41 +383,38 @@
 
         @pl.when(jnp.logical_and(passes[side], g < G - 1))
         def _():
-            @pl.loop(0, NEAR_CHUNKS)
-            def _(c):
-                y_copy(side, c).wait_send()
+            y_copy(side, 0).wait_send()
+            y_copy(side, 1).wait_send()
 
         @pl.when(jnp.logical_and(passes[side], g < G - 2))
         def _():
-            for c in range(FAR_CHUNKS):
-                y_copy(side, c, True).wait_send()
+            y_copy(side, 2).wait_send()
 
         @pl.when(jnp.logical_and(middle[side], g > 0))
         def _():
-            near_edge(side).wait_send()
+            near_halo(side).wait_send()
 
         @pl.when(jnp.logical_and(middle[side], g > 1))
         def _():
-            relay_edge(side).wait_send()
+            relay_halo(side).wait_send()
 
         @pl.when(jnp.logical_and(middle[side], relays))
         def _():
-            far_edge(side).wait_send()
+            far_halo(side).wait_send()
 
     @pl.when(g > 0)
     def _():
-        @pl.loop(0, NEAR_CHUNKS)
-        def _(c):
-            x_copy(c).wait_send()
-
-    for c in range(FAR_CHUNKS):
+        for part in range(8):
+            near(part).wait_send()
+
+    for part in range(3):
         @pl.when(g > 1)
         def _():
-            relay_copy(c).wait_send()
+            relay(part).wait_send()
 
         @pl.when(relays)
         def _():
-            far_copy(c).wait_send()
+            far(part).wait_send()
 
 
 def solution(mesh):
@@ -456,8 +437,8 @@
                 pltpu.VMEM((3, FAR, COLS, 128), jnp.float32),
                 pltpu.VMEM((3, FAR, 8, 128), jnp.float32),
                 pltpu.SMEM((STEPS + 1,), jnp.int32),
-                dma((2,)), dma((CHUNKS,)), dma((CHUNKS,)), dma((FAR_CHUNKS,)), dma((FAR_CHUNKS,)),
-                dma((2, CHUNKS + 1)), dma((2, CHUNKS + 1)), dma((2,)), dma((2,)), dma((3,)), dma((3,)),
+                dma((2,)), dma((8,)), dma((8,)), dma((3,)), dma((3,)), dma((3,)), dma((3,)),
+                dma((2, 4)), dma((2, 4)), dma((2,)), dma((2,)), dma((3,)), dma((3,)),
             ],
             compiler_params=pltpu.CompilerParams(
                 collective_id=0, has_side_effects=True, vmem_limit_bytes=60 * 1024 * 1024),

time: 58.4 us -> 47.3 us (0.81)
  the two profiles are of different devices: /device:TPU:17 before, /device:TPU:25 now
where the time goes in v6:
time: 47.3 us; the launch traced here: 47.2 us
  Pallas kernels  45.1 us (95%)
  local copies, waits for them, and re-layouts  2.06 us (4%)
    pallas_call x1, Pallas kernels, body(): pl.pallas_call(functools.partial(kernel, G, W), out_shape=jax.ShapeDtypeS...  45.1 us
    unnamed x1, local copies, waits for them, and re-layouts  2.06 us

profile of v6, /device:TPU:25, one launch (start us, length us, event | category | flops | bytes accessed | tf_op | source)
XLA Modules:
  0.0 47.2 jit_solution(6128786391497202943)
XLA Ops:
  0.0 45.1 %shard_map.37 = f32[3,16,32,128]{3,2,1,0:T(8,128)} custom-call(s32[8]{0:T(128)} %slide.1, f32[3,16,32,128]{3,2,1,0:T(8,128)} %fields.1, f32[3,16,32,128]{3,2,1,0:T(8,128)} %melt.1), custom_call_target="tpu_custom_call" | custom-call | tf_op jit(solution)/shard_map/pallas_call | solution.py:425
  45.1 2.1 %copy.5 = f32[3,16,32,128]{3,2,1,0:T(8,128)} copy(f32[3,16,32,128]{3,2,1,0:T(8,128)} %shard_map.37) | data formatting | bytes 1572864

commit v7 on v6

--- a/solution.py
+++ b/solution.py
@@ -125,8 +125,9 @@
     def halo(first, planes, side):
         return lev.at[0, :, pl.ds(PAD + first, planes), pl.ds((LO + COLS, LO - 8)[side], 8), :]
 
-    def near_halo(side):
-        return remote(halo(0, OWN, side), halo(OWN, OWN, side), (e_send, e_recv), 0, {"grow": g - 1})
+    def near_halo(side, half):
+        first = HALF * half
+        return remote(halo(first, HALF, side), halo(OWN + first, HALF, side), (e_send, e_recv), 3 * half, {"grow": g - 1})
 
     def relay_halo(side):
         return remote(halo(0, FAR, side), ebuf, (e_send, e_recv), 1, {"grow": relay_to})
@@ -286,7 +287,8 @@
     for side in (0, 1):
         @pl.when(jnp.logical_and(middle[side], g > 0))
         def _():
-            near_halo(side).start()
+            near_halo(side, 0).start()
+            near_halo(side, 1).start()
             for part in range(6, 8):
                 near(part).start()
 
@@ -341,9 +343,10 @@
             far_edges()
 
         for side in (0, 1):
-            @pl.when(jnp.logical_and(jnp.logical_and(stage == 0, g < G - 1), middle[side]))
-            def _():
-                near_halo(side).wait_recv()
+            for half in (0, 1):
+                @pl.when(jnp.logical_and(jnp.logical_and(stage == 2 * half, g < G - 1), middle[side]))
+                def _():
+                    near_halo(side, half).wait_recv()
 
         @pl.when(jnp.logical_and(stage == 4, g < G - 2))
         def _():
@@ -392,7 +395,8 @@
 
         @pl.when(jnp.logical_and(middle[side], g > 0))
         def _():
-            near_halo(side).wait_send()
+            near_halo(side, 0).wait_send()
+            near_halo(side, 1).wait_send()
 
         @pl.when(jnp.logical_and(middle[side], g > 1))
         def _():
@@ -427,8 +431,8 @@
             out_shape=jax.ShapeDtypeStruct(fields.shape, jnp.float32),
             in_specs=[
                 pl.BlockSpec(memory_space=pltpu.SMEM),
-                pl.BlockSpec(memory_space=pl.ANY),
-                pl.BlockSpec(memory_space=pl.ANY),
+                pl.BlockSpec(memory_space=pltpu.HBM),
+                pl.BlockSpec(memory_space=pltpu.HBM),
             ],
             out_specs=pl.BlockSpec(memory_space=pltpu.VMEM),
             scratch_shapes=[
@@ -438,10 +442,10 @@
                 pltpu.VMEM((3, FAR, 8, 128), jnp.float32),
                 pltpu.SMEM((STEPS + 1,), jnp.int32),
                 dma((2,)), dma((8,)), dma((8,)), dma((3,)), dma((3,)), dma((3,)), dma((3,)),
-                dma((2, 4)), dma((2, 4)), dma((2,)), dma((2,)), dma((3,)), dma((3,)),
+                dma((2, 4)), dma((2, 4)), dma((2,)), dma((2,)), dma((4,)), dma((4,)),
             ],
             compiler_params=pltpu.CompilerParams(
-                collective_id=0, has_side_effects=True, vmem_limit_bytes=60 * 1024 * 1024),
+                collective_id=0, has_side_effects=True, vmem_limit_bytes=54000 * 1024),
         )(slide_planes, fields, melt_planes)
 
     return jax.shard_map(

time: 47.3 us -> 45.8 us (0.968)
  Pallas kernels: 45.1 us -> 44.2 us
  local copies, waits for them, and re-layouts: 2.06 us -> 1.54 us
    pallas_call x1, Pallas kernels: 45.1 us -> 44.2 us  [body(): pl.pallas_call(functools.partial(kernel, G, W), out_shape=jax.ShapeDtypeS...]
    unnamed x1 -> x3, local copies, waits for them, and re-layouts: 2.06 us -> 1.54 us
where the time goes in v7:
time: 45.8 us; the launch traced here: 45.7 us
  Pallas kernels  44.2 us (97%)
  local copies, waits for them, and re-layouts  1.54 us (3%)
    pallas_call x1, Pallas kernels, body(): pl.pallas_call(functools.partial(kernel, G, W), out_shape=jax.ShapeDtypeS...  44.2 us
    unnamed x3, local copies, waits for them, and re-layouts  1.54 us

profile of v7, /device:TPU:25, one launch (start us, length us, event | category | flops | bytes accessed | tf_op | source)
XLA Modules:
  0.0 45.7 jit_solution(16887679715316575236)
XLA Ops:
  0.0 0.0 copy-start
  0.0 0.7 %copy-done = s32[8]{0:T(128)S(1)} copy-done((s32[8]{0:T(128)S(1)}, s32[8]{0:T(128)}, u32[]{:S(2)}) %copy-start) | copy-done | bytes 56
  0.7 44.2 %shard_map.37 = f32[3,16,32,128]{3,2,1,0:T(8,128)S(1)} custom-call(s32[8]{0:T(128)S(1)} %copy-done, f32[3,16,32,128]{3,2,1,0:T(8,128)} %fields.1, f32[3,16,32,128]{3,2,1,0:T(8,128)} %melt.1), custom_call_target="tpu_custom_call" | custom-call | tf_op jit(solution)/shard_map/pallas_call | solution.py:429
  44.8 0.9 %copy.5 = f32[3,16,32,128]{3,2,1,0:T(8,128)} copy(f32[3,16,32,128]{3,2,1,0:T(8,128)S(1)} %shard_map.37) | data formatting | bytes 1572864
Async XLA Ops:
  0.0 0.7 %copy-start = (s32[8]{0:T(128)S(1)}, s32[8]{0:T(128)}, u32[]{:S(2)}) copy-start(s32[8]{0:T(128)} %slide.1) | copy-start | bytes 100

commit v8 on v7

--- a/solution.py
+++ b/solution.py
@@ -223,7 +223,9 @@
     span = pl.ds(LO - 8, COLS + 16)
 
     def left_edge(t, x, n):
-        @pl.when(jnp.logical_and(g == 0, x < OWN))
+        reach = jnp.where(t == 0, -OWN, jnp.where(t < 3, OWN // 2, OWN))
+
+        @pl.when(jnp.logical_and(g == 0, x < reach))
         def _():
             for q in range(n):
                 keep = x + q >= cur[t + 1]

time: 45.8 us -> 45.4 us (level)
  no operation moved by 1% of the time
where the time goes in v8:
time: 45.4 us
  Pallas kernels  43.8 us (96%)
  local copies, waits for them, and re-layouts  1.54 us (3%)
    pallas_call x1, Pallas kernels, body(): pl.pallas_call(functools.partial(kernel, G, W), out_shape=jax.ShapeDtypeS...  43.8 us
    unnamed x3, local copies, waits for them, and re-layouts  1.54 us

profile of v8, /device:TPU:25, one launch (start us, length us, event | category | flops | bytes accessed | tf_op | source)
XLA Modules:
  0.0 45.4 jit_solution(1107092019219947607)
XLA Ops:
  0.0 0.0 copy-start
  0.0 0.7 %copy-done = s32[8]{0:T(128)S(1)} copy-done((s32[8]{0:T(128)S(1)}, s32[8]{0:T(128)}, u32[]{:S(2)}) %copy-start) | copy-done | bytes 56
  0.7 43.8 %shard_map.37 = f32[3,16,32,128]{3,2,1,0:T(8,128)S(1)} custom-call(s32[8]{0:T(128)S(1)} %copy-done, f32[3,16,32,128]{3,2,1,0:T(8,128)} %fields.1, f32[3,16,32,128]{3,2,1,0:T(8,128)} %melt.1), custom_call_target="tpu_custom_call" | custom-call | tf_op jit(solution)/shard_map/pallas_call | solution.py:431
  44.5 0.9 %copy.5 = f32[3,16,32,128]{3,2,1,0:T(8,128)} copy(f32[3,16,32,128]{3,2,1,0:T(8,128)S(1)} %shard_map.37) | data formatting | bytes 1572864
Async XLA Ops:
  0.0 0.7 %copy-start = (s32[8]{0:T(128)S(1)}, s32[8]{0:T(128)}, u32[]{:S(2)}) copy-start(s32[8]{0:T(128)} %slide.1) | copy-start | bytes 100

commit v9 on v8

--- a/solution.py
+++ b/solution.py
@@ -164,7 +164,12 @@
 
     pl.semaphore_wait(barrier, count)
     for side in (0, 1):
-        @pl.when(sends[side])
+        @pl.when(middle[1 - side])
+        def _():
+            y_own(side).start()
+
+    for side in (0, 1):
+        @pl.when(passes[side])
         def _():
             y_own(side).start()
 

time: 45.4 us -> 45.4 us (level)
  no operation moved by 1% of the time
where the time goes in v9:
time: 45.4 us
  Pallas kernels  43.8 us (96%)
  local copies, waits for them, and re-layouts  1.54 us (3%)
    pallas_call x1, Pallas kernels, body(): pl.pallas_call(functools.partial(kernel, G, W), out_shape=jax.ShapeDtypeS...  43.8 us
    unnamed x3, local copies, waits for them, and re-layouts  1.54 us

profile of v9, /device:TPU:25, one launch (start us, length us, event | category | flops | bytes accessed | tf_op | source)
XLA Modules:
  0.0 45.4 jit_solution(9054919063131233460)
XLA Ops:
  0.0 0.0 copy-start
  0.0 0.7 %copy-done = s32[8]{0:T(128)S(1)} copy-done((s32[8]{0:T(128)S(1)}, s32[8]{0:T(128)}, u32[]{:S(2)}) %copy-start) | copy-done | bytes 56
  0.7 43.8 %shard_map.37 = f32[3,16,32,128]{3,2,1,0:T(8,128)S(1)} custom-call(s32[8]{0:T(128)S(1)} %copy-done, f32[3,16,32,128]{3,2,1,0:T(8,128)} %fields.1, f32[3,16,32,128]{3,2,1,0:T(8,128)} %melt.1), custom_call_target="tpu_custom_call" | custom-call | tf_op jit(solution)/shard_map/pallas_call | solution.py:436
  44.5 0.9 %copy.5 = f32[3,16,32,128]{3,2,1,0:T(8,128)} copy(f32[3,16,32,128]{3,2,1,0:T(8,128)S(1)} %shard_map.37) | data formatting | bytes 1572864
Async XLA Ops:
  0.0 0.7 %copy-start = (s32[8]{0:T(128)S(1)}, s32[8]{0:T(128)}, u32[]{:S(2)}) copy-start(s32[8]{0:T(128)} %slide.1) | copy-start | bytes 100
